TPU v7x, 512 devices: a whole 4x4x16 slice. The times are simulated.
512 devices in a mesh: row: 4 (over x), col: 8 (over y, core), layer: 16 (over z).
Axes of the slice: x: 4, y: 4, z: 16, core: 2. Of those that a mesh axis runs over, the one named last changes fastest.
Arguments:
- a_blocks: bfloat16 [16, 2, 64, 64, 512], P('layer', None, ('row', 'col')), may hold values from -0.046875 to 0.046875
- a_cols: int32 [16, 2, 64, 8], P('layer', None, ('row', 'col')), may hold values from 0 to 7
- p_blocks: bfloat16 [16, 2, 8, 8, 64, 256], P('layer', None, 'col', 'row'), may hold values from -12 to 12
- p_cols: int32 [16, 2, 8, 8, 4], P('layer', None, 'col', 'row'), may hold values from 0 to 15, as said below
- c_cols: int32 [8, 64, 8], P('col', 'row'), may hold values from 0 to 15, as said below
Outputs:
- c_blocks: bfloat16 [8, 64, 64, 512], P('col', ('row', 'layer'))
Inputs may be any that keep to these rules, and one draw needn't show every extreme that they name: `p_cols`: the 4 entries of a block row of P in one column group are distinct. `c_cols`: the 8 entries of a block row of C in one column group are distinct.
All inputs are finite; a program needn't handle non-finite values.
Results may differ from a plain program's by a relative error of at most 0.008.
Values may be sent and summed in bfloat16 or wider, within the bound.
No kernel may reach another device: no remote copies, remote signals or barrier semaphores. Data moves between devices by JAX's collectives and lax.ppermute only.
A program may use at most 64 MiB of HBM per device.

v0:
```python
import jax
import jax.numpy as jnp
from jax import lax
from jax.sharding import PartitionSpec as P

SECTIONS = 2


def block_terms(a_strip, row_idx, p_panel, panel_idx, targets):
    row_count = a_strip.shape[0]
    side = a_strip.shape[1]
    couple = row_idx.shape[1]
    fine_slots = panel_idx.shape[1]
    coarse_slots = targets.shape[1]
    picked = p_panel[row_idx]
    a_four = a_strip.reshape(row_count, side, couple, side)
    prods = jnp.einsum("ixky,ikyz->ikxz", a_four, picked, preferred_element_type=jnp.float32)
    prods = prods.reshape(row_count, couple, side, fine_slots, side)
    coarse = panel_idx[row_idx]
    onehot = (coarse[:, :, :, None] == targets[:, None, None, :]).astype(jnp.float32)
    placed = jnp.einsum("ikxjz,ikjm->ixmz", prods, onehot, preferred_element_type=jnp.float32)
    return placed.reshape(row_count, side, coarse_slots * side)


def local(a_blocks, a_cols, p_blocks, p_cols, c_cols):
    targets = c_cols[0]
    group_rows = targets.shape[0]
    side = a_blocks.shape[3]
    gathered = []
    for section_no in range(SECTIONS):
        a_strip, row_idx = (
            lax.all_gather(a_blocks[0, section_no], "col", axis=0, tiled=True),
            lax.all_gather(a_cols[0, section_no], "col", axis=0, tiled=True),
        )
        p_panel, panel_idx = (
            lax.all_gather(p_blocks[0, section_no, 0], "row", axis=0, tiled=True),
            lax.all_gather(p_cols[0, section_no, 0], "row", axis=0, tiled=True),
        )
        gathered.append((a_strip, row_idx, p_panel, panel_idx))
    own_rows = group_rows // lax.axis_size("layer")
    running = jnp.zeros(
        (lax.axis_size("layer") * own_rows, side, targets.shape[1] * side), jnp.float32
    )
    for a_strip, row_idx, p_panel, panel_idx in gathered:
        running = running + block_terms(a_strip, row_idx, p_panel, panel_idx, targets)
    shares = lax.psum_scatter(running, "layer", scatter_dimension=0, tiled=True)
    return shares.astype(jnp.bfloat16)[None]


def solution(mesh):
    return jax.shard_map(
        local,
        mesh=mesh,
        in_specs=(
            P("layer", None, ("row", "col"), None, None),
            P("layer", None, ("row", "col"), None),
            P("layer", None, "col", "row", None, None),
            P("layer", None, "col", "row", None),
            P("col", "row", None),
        ),
        out_specs=P("col", ("row", "layer"), None, None),
        check_vma=False,
    )
```

profile of v0, /device:TPU:2, one launch (start us, length us, event | category | flops | bytes accessed | tf_op | source)
XLA Modules:
  0.0 225.8 jit_solution(7127737911896459356)
XLA Ops:
  6.5 1.7 slice_bitcast_fusion.1
  8.3 0.7 all-gather.11.cloned.1.call-update
  9.0 0.7 fusion.17
  9.7 12.8 %all-gather.4 = s32[1,1,1,8,4]{4,2,1,0,3:T(1,128)S(1)} all-gather(s32[1,1,1,2,4]{4,2,1,0,3:T(1,128)S(1)} %bitcast.78), channel_id=6, replica_groups=mesh['row'=4,'col'=8,'layer'=16] {'row'}, dimensions={3}, use_global_device_ids=true | all-gather | bytes 160 | tf_op jit(solution)/shard_map/all_gather | solution.py:37
  22.6 7.0 %all-gather = s32[1,1,1,8,4]{4,2,1,0,3:T(1,128)S(1)} all-gather(s32[1,1,1,2,4]{4,2,1,0,3:T(1,128)S(1)} %bitcast.77), channel_id=2, replica_groups=mesh['row'=4,'col'=8,'layer'=16] {'row'}, dimensions={3}, use_global_device_ids=true | all-gather | bytes 160 | tf_op jit(solution)/shard_map/all_gather | solution.py:37
  29.6 0.7 fusion.18
  30.3 8.2 %all-gather.5 = s32[1,1,16,8]{3,1,0,2:T(1,128)S(1)} all-gather(s32[1,1,2,8]{3,1,0,2:T(1,128)S(1)} %bitcast.79), channel_id=7, replica_groups=mesh['row'=4,'col'=8,'layer'=16] {'col'}, dimensions={2}, use_global_device_ids=true | all-gather | bytes 576 | tf_op jit(solution)/shard_map/all_gather | solution.py:33
  38.5 0.1 copy.50
  38.6 0.1 reshape.40
  38.7 0.9 slice_bitcast_fusion.3
  39.6 11.0 %all-gather.6 = bf16[1,1,1,8,64,256]{5,4,2,1,0,3:T(8,128)(2,1)S(1)} all-gather(bf16[1,1,1,2,64,256]{5,4,2,1,0,3:T(8,128)(2,1)S(1)} %get-tuple-element.8), channel_id=8, replica_groups=mesh['row'=4,'col'=8,'layer'=16] {'row'}, dimensions={3}, use_global_device_ids=true | all-gather | bytes 327680 | tf_op jit(solution)/shard_map/all_gather | solution.py:36
  50.6 2.8 %gather_fusion.3 = bf16[128,64,256]{2,1,0:T(8,128)(2,1)} fusion(bf16[8,64,256]{2,1,0:T(8,128)(2,1)S(1)} %bitcast.67, s32[1024]{0:T(1024)S(1)} %pad_clamp_fusion), kind=kCustom, calls=%fused_computation.3 | custom fusion | bytes 8389120 | tf_op jit(solution)/shard_map/gather | solution.py:15
  53.4 0.6 gather_fusion.2
  54.1 0.2 copy.52
  54.3 9.4 %all-gather.1 = s32[1,1,16,8]{3,1,0,2:T(1,128)S(1)} all-gather(s32[1,1,2,8]{3,1,0,2:T(1,128)S(1)} %bitcast.76), channel_id=3, replica_groups=mesh['row'=4,'col'=8,'layer'=16] {'col'}, dimensions={2}, use_global_device_ids=true | all-gather | bytes 576 | tf_op jit(solution)/shard_map/all_gather | solution.py:33
  63.8 0.1 copy.38
  63.9 0.1 reshape.24
  64.0 12.3 %all-gather.2 = bf16[1,1,1,8,64,256]{5,4,2,1,0,3:T(8,128)(2,1)S(1)} all-gather(bf16[1,1,1,2,64,256]{5,4,2,1,0,3:T(8,128)(2,1)S(1)} %get-tuple-element.7), channel_id=4, replica_groups=mesh['row'=4,'col'=8,'layer'=16] {'row'}, dimensions={3}, use_global_device_ids=true | all-gather | bytes 327680 | tf_op jit(solution)/shard_map/all_gather | solution.py:36
  76.3 2.8 %gather_fusion.1 = bf16[128,64,256]{2,1,0:T(8,128)(2,1)} fusion(bf16[8,64,256]{2,1,0:T(8,128)(2,1)S(1)} %bitcast.68, s32[1024]{0:T(1024)S(1)} %pad_clamp_fusion.1), kind=kCustom, calls=%fused_computation.1 | custom fusion | bytes 8389120 | tf_op jit(solution)/shard_map/gather | solution.py:15
  79.0 0.6 gather_fusion
  79.7 0.2 copy.40
  79.9 2.8 %reshape.20 = bf16[16,64,8,64]{3,2,1,0:T(8,128)(2,1)S(1)} reshape(bf16[1,1,16,64,512]{4,3,1,0,2:T(8,128)(2,1)} %all-gather.13.cloned.1.call-done) | data formatting | bytes 2097152 | tf_op jit(solution)/shard_map/reshape | solution.py:16
  82.7 5.3 %convolution_bitcast_fusion = bf16[16,8,64,256]{3,2,1,0:T(8,128)(2,1)} fusion(bf16[16,8,64,256]{3,2,1,0:T(8,128)(2,1)} %bitcast.71, bf16[16,64,8,64]{3,2,1,0:T(8,128)(2,1)S(1)} %reshape.20), kind=kOutput, calls=%fused_computation.10 | convolution fusion | flops 268435456 | bytes 9437184 | tf_op jit(solution)/shard_map/ixky,ikyz->ikxz/dot_general | solution.py:17
  88.0 12.9 %reshape.21 = bf16[16,8,64,4,64]{4,3,2,1,0:T(4,128)(2,1)} reshape(bf16[16,8,64,256]{3,2,1,0:T(8,128)(2,1)} %convolution_bitcast_fusion) | data formatting | bytes 8388608 | tf_op jit(solution)/shard_map/reshape | solution.py:18
  100.9 2.8 %reshape.18 = bf16[16,64,8,64]{3,2,1,0:T(8,128)(2,1)S(1)} reshape(bf16[1,1,16,64,512]{4,3,1,0,2:T(8,128)(2,1)} %all-gather.11.cloned.1.call-done) | data formatting | bytes 2097152 | tf_op jit(solution)/shard_map/reshape | solution.py:16
  103.7 5.4 %convolution_bitcast_fusion.1 = bf16[16,8,64,256]{3,2,1,0:T(8,128)(2,1)} fusion(bf16[16,8,64,256]{3,2,1,0:T(8,128)(2,1)} %bitcast.72, bf16[16,64,8,64]{3,2,1,0:T(8,128)(2,1)S(1)} %reshape.18), kind=kOutput, calls=%fused_computation.11 | convolution fusion | flops 268435456 | bytes 9437184 | tf_op jit(solution)/shard_map/ixky,ikyz->ikxz/dot_general | solution.py:17
  109.1 12.9 %reshape.19 = bf16[16,8,64,4,64]{4,3,2,1,0:T(4,128)(2,1)} reshape(bf16[16,8,64,256]{3,2,1,0:T(8,128)(2,1)} %convolution_bitcast_fusion.1) | data formatting | bytes 8388608 | tf_op jit(solution)/shard_map/reshape | solution.py:18
  122.0 8.5 %fusion = f32[16,8,64,64,1]{3,1,4,2,0:T(8,128)S(1)} fusion(bf16[16,8,64,4,64]{4,3,2,1,0:T(4,128)(2,1)} %reshape.21, s32[16,8,4]{1,2,0:T(4,128)S(1)} %copy.52, s32[16,8]{1,0:T(8,128)S(1)} %copy.41), kind=kOutput, calls=%fused_computation.4 | convolution fusion | flops 33558528 | bytes 6294016 | tf_op jit(solution)/shard_map/ikxjz,ikjm->ixmz/dot_general | solution.py:21
  130.5 6.7 %fusion.4 = f32[16,64,8,64]{3,2,1,0:T(8,128)} fusion(f32[16,8,64,64,1]{3,1,4,2,0:T(8,128)S(1)} %fusion, bf16[16,8,64,4,64]{4,3,2,1,0:T(4,128)(2,1)S(1)} %copy-done, s32[16,8]{1,0:T(8,128)S(1)} %copy.41, s32[16,8,4]{1,2,0:T(4,128)S(1)} %copy.40), kind=kOutput, calls=%fused_computation.9 | convolution fusion | flops 34082816 | bytes 8391168 | tf_op jit(solution)/shard_map/ikxjz,ikjm->ixmz/dot_general | solution.py:21
  137.2 4.8 %add.23 = f32[16,64,512]{2,1,0:T(8,128)} reshape(f32[16,64,8,64]{3,2,1,0:T(8,128)} %fusion.4) | data formatting | bytes 4194304 | tf_op jit(solution)/shard_map/add | solution.py:45
  142.0 75.7 %reduce-scatter.2.cloned.1.call-done = f32[1,64,512]{2,1,0:T(8,128)} async-done(((f32[16,64,512]{2,1,0:T(8,128)}), f32[1,64,512]{2,1,0:T(8,128)}) %reduce-scatter.2.cloned.1.call-update) | async-done | bytes 131088 | tf_op jit(solution)/shard_map/reduce_scatter | solution.py:46
  217.7 1.5 convert_bitcast_fusion
  (18 shorter events, 0.4 us)
Async XLA Ops:
  6.5 73.3 %all-gather.13.cloned.1.call-start = ((), (), s32[]{:S(2)}) async-start(), calls=%async_computation.3 | async-start | bytes 1179648 | tf_op jit(solution)/shard_map/all_gather | solution.py:32
  8.2 92.7 %all-gather.11.cloned.1.call-start = ((), (), s32[]{:S(2)}) async-start(), calls=%async_computation.2 | async-start | bytes 1179648 | tf_op jit(solution)/shard_map/all_gather | solution.py:32
  9.0 208.7 %reduce-scatter.2.cloned.1.call-start = ((), (), s32[]{:S(2)}) async-start(), calls=%async_computation.1 | async-start | bytes 2228224 | tf_op jit(solution)/shard_map/reduce_scatter | solution.py:46
  50.6 3.6 %copy-start.1 = (s32[1,16,8]{1,2,0:T(8,128)S(1)}, s32[1,16,8]{1,2,0:T(8,128)}, u32[]{:S(2)}) copy-start(s32[1,16,8]{1,2,0:T(8,128)} %param.9) | copy-start | bytes 1540
  122.0 8.5 %copy-start = (bf16[16,8,64,4,64]{4,3,2,1,0:T(4,128)(2,1)S(1)}, bf16[16,8,64,4,64]{4,3,2,1,0:T(4,128)(2,1)}, u32[]{:S(2)}) copy-start(bf16[16,8,64,4,64]{4,3,2,1,0:T(4,128)(2,1)} %reshape.19) | copy-start | bytes 12582916
Sparse Core Ops, SparseCore 0:
  9.5 35.3 all-gather.12
  47.1 30.9 all-gather.10
  142.1 75.5 reduce-scatter.1
where the time goes:
time: 227 us; the launch traced here: 226 us
  waiting for transfers between devices  76.5 us (34%)
  blocking collectives  60.8 us (27%)
  local copies, waits for them, and re-layouts  47.8 us (21%)
  matrix products  25.9 us (11%)
  between operations  13.2 us (6%)
    reduce_scatter x1, waiting for transfers between devices, local(): shares = lax.psum_scatter(running, 'layer', scatter_dimension=0, tiled=True)  75.7 us
    reshape x2, local copies, waits for them, and re-layouts, block_terms(): prods = prods.reshape(row_count, couple, side, fine_slots, side)  25.8 us
    all_gather x2, blocking collectives, local(): lax.all_gather(p_blocks[0, section_no, 0], 'row', axis=0, tiled=True)  23.3 us
    all_gather x2, blocking collectives, local(): lax.all_gather(p_cols[0, section_no, 0], 'row', axis=0, tiled=True)  19.8 us
    all_gather x2, blocking collectives, local(): lax.all_gather(a_cols[0, section_no], 'col', axis=0, tiled=True)  17.6 us
    dot_general x2, matrix products, block_terms(): jnp.einsum('ikxjz,ikjm->ixmz', prods, onehot, preferred_element_type=jnp....  15.2 us
    dot_general x2, matrix products, block_terms(): jnp.einsum('ixky,ikyz->ikxz', a_four, picked, preferred_element_type=jnp....  10.7 us
    reshape x2, local copies, waits for them, and re-layouts, block_terms(): a_four = a_strip.reshape(row_count, side, couple, side)  5.58 us
  transfers between devices with their start and end apart: 3, of which 1 were waited for; matrix products, arithmetic and copies ran while one was open for 14% of the time, Pallas kernels for 0%

commit v1 on v0

v1 whole, which is shorter than its diff:
```python
import jax
import jax.numpy as jnp
from jax import lax
from jax.experimental import pallas as pl
from jax.experimental.pallas import tpu as pltpu
from jax.sharding import PartitionSpec as P


BLK = 64
KS = 8
KP = 4
KC = 8
NCC = 16
SEC = 2
OWN = 2
IBS = 8
CORES = 2
HEAD = 16
BODY = SEC * OWN * BLK
PAIR = 2 * BLK
SMALL = 8 * 1024 * 1024
STEP = 16
VMEM = pl.BlockSpec(memory_space=pltpu.VMEM)
SMEM = pl.BlockSpec(memory_space=pltpu.SMEM)


def repeat(count, unroll, step):
    def several(t, _):
        for u in range(unroll):
            step(t * unroll + u)
        return 0

    lax.fori_loop(0, count // unroll, several, 0)


def head_row(values):
    lane = lax.broadcasted_iota(jnp.int32, (HEAD, PAIR), 1)
    row = jnp.zeros((HEAD, PAIR), jnp.float32)
    for n, value in enumerate(values):
        row = jnp.where(lane == n, value.astype(jnp.float32), row)
    return row.astype(jnp.bfloat16)


def pack_kernel(a_cols, p_cols, a_blocks, p_blocks, a_out, p_out):
    a_head = head_row([a_cols[0, s, j, k] for s in range(SEC) for j in range(OWN) for k in range(KS)])
    p_head = head_row([p_cols[0, s, 0, j, q] for s in range(SEC) for j in range(OWN) for q in range(KP)])
    for n in range(a_out.shape[0]):
        a_out[n, :BODY, :] = a_blocks[...]
        a_out[n, BODY:, :] = jnp.zeros((HEAD, KS * BLK), jnp.bfloat16)
        a_out[n, BODY:, :PAIR] = a_head
    p_out[:BODY, :] = p_blocks[...]
    p_out[BODY:, :] = jnp.zeros((HEAD, KP * BLK), jnp.bfloat16)
    p_out[BODY:, :PAIR] = p_head


def twins(two):
    turned = pltpu.roll(two, BLK, 1)
    low = lax.broadcasted_iota(jnp.int32, two.shape, 1) < BLK
    return jnp.where(low, two, turned), jnp.where(low, turned, two)


def copies_of(tile):
    found = []
    for t in range(tile.shape[1] // PAIR):
        found.extend(twins(tile[:, t * PAIR : (t + 1) * PAIR].astype(jnp.float32)))
    return found


def swap(tile):
    return jnp.concatenate([tile[:, BLK:], tile[:, :BLK]], axis=1)


def masks_of(head, first, count, pairs):
    place = (lax.broadcasted_iota(jnp.int32, (STEP, PAIR), 1) // BLK).astype(jnp.float32)
    cols = [jnp.broadcast_to(head[:, first + n : first + n + 1], (STEP, PAIR)) for n in range(count)]
    return [[place + 2 * pair == col for col in cols] for pair in range(pairs)]


def expand_kernel(own, *refs):
    p_parts, wide = refs[:-1], refs[-1]
    for d, p_ref in enumerate(p_parts):
        src = lax.rem(own[1] - d + len(p_parts), len(p_parts))
        head = p_ref[BODY:, :PAIR].astype(jnp.float32)
        for n in range(SEC * OWN):
            s, j = n // OWN, n % OWN
            masks = masks_of(head, n * KP, KP, NCC // 2)
            slab = pl.multiple_of((s * IBS + src * OWN + j) * BLK, BLK)
            for g in range(BLK // STEP):
                copies = copies_of(p_ref[n * BLK + g * STEP : n * BLK + (g + 1) * STEP, :])
                for pair in range(NCC // 2):
                    acc = jnp.where(masks[pair][0], copies[0], 0.0)
                    for q in range(1, KP):
                        acc = jnp.where(masks[pair][q], copies[q], acc)
                    wide[pl.ds(slab + g * STEP, STEP), pair * PAIR : (pair + 1) * PAIR] = acc.astype(jnp.bfloat16)


def product_kernel(near, side, own, a_ref, wide, *refs):
    out, rows, full = refs[-3:]
    owner = own[0] if side == 0 else 1 - own[0]
    parts = a_ref.shape[0]
    c_at = 2

    def gather(src):
        head = a_ref[src, BODY:, :PAIR].astype(jnp.float32)
        for j in range(OWN):
            row = pl.multiple_of((src * OWN + j) * BLK, BLK)
            for s in range(SEC):
                masks = masks_of(head, (s * OWN + j) * KS, KS, IBS // 2)
                for g in range(BLK // STEP):
                    first = (s * OWN + j) * BLK + g * STEP
                    copies = copies_of(a_ref[src, first : first + STEP, :])
                    for pair in range(IBS // 2):
                        acc = jnp.where(masks[pair][0], copies[0], 0.0)
                        for k in range(1, KS):
                            acc = acc + jnp.where(masks[pair][k], copies[k], 0.0)
                        lanes = slice((s * IBS // 2 + pair) * PAIR, (s * IBS // 2 + pair + 1) * PAIR)
                        rows[pl.ds(row + g * STEP, STEP), lanes] = acc.astype(jnp.bfloat16)

    repeat(parts, 2, gather)
    full[...] = jnp.dot(rows[...], wide[...], preferred_element_type=jnp.float32).astype(jnp.bfloat16)
    low = lax.broadcasted_iota(jnp.int32, (BLK, PAIR), 1).astype(jnp.int16) < jnp.int16(BLK)

    def pick(n):
        i = (n // OWN * CORES + owner) * OWN + lax.rem(n, OWN)
        row = pl.multiple_of(n * BLK, BLK)
        for pair in range(KC // 2):
            picked = []
            for m in range(2):
                c = own[c_at + i * KC + pair * 2 + m]
                two = full[pl.ds(row, BLK), pl.ds(pl.multiple_of(c // 2 * PAIR, PAIR), PAIR)]
                picked.append(jnp.where(lax.rem(c, 2) == m, two, swap(two)))
            out[lax.rem(i, near), i // near, :, pair * PAIR : (pair + 1) * PAIR] = jnp.where(low, *picked)

    repeat(parts * OWN, 8, pick)


def local(a_blocks, a_cols, p_blocks, p_cols, c_cols):
    rows, chips, layers = lax.axis_size("row"), lax.axis_size("chip"), lax.axis_size("layer")
    near = 4
    a_out, p_out = pl.pallas_call(
        pack_kernel,
        out_shape=(
            jax.ShapeDtypeStruct((chips, BODY + HEAD, KS * BLK), jnp.bfloat16),
            jax.ShapeDtypeStruct((BODY + HEAD, KP * BLK), jnp.bfloat16),
        ),
        in_specs=[SMEM, SMEM, VMEM, VMEM],
        out_specs=(VMEM, VMEM),
    )(a_cols, p_cols, a_blocks.reshape(BODY, KS * BLK), p_blocks.reshape(BODY, KP * BLK))
    a_own = lax.all_to_all(a_out, "chip", 0, 0, tiled=True)
    p_parts = [p_out] + [lax.ppermute(p_out, "row", [(i, (i + d) % rows) for i in range(rows)]) for d in range(1, rows)]
    a_other = lax.ppermute(a_own, "core", [(0, 1), (1, 0)])
    own = jnp.stack([lax.axis_index("core"), lax.axis_index("row")]).astype(jnp.int32)
    own = jnp.concatenate([own, c_cols.reshape(-1)])
    wide = pl.pallas_call(
        expand_kernel,
        out_shape=jax.ShapeDtypeStruct((SEC * IBS * BLK, NCC * BLK), jnp.bfloat16),
        in_specs=[SMEM] + [VMEM] * rows,
        out_specs=VMEM,
        cost_estimate=pl.CostEstimate(flops=10**6, bytes_accessed=3 * 10**6, transcendentals=0),
        compiler_params=pltpu.CompilerParams(vmem_limit_bytes=SMALL),
    )(own, *p_parts)

    def products(side, part_of_a, *so_far):
        return pl.pallas_call(
            lambda *refs: product_kernel(near, side, *refs),
            out_shape=jax.ShapeDtypeStruct((near, layers // near, BLK, KC * BLK), jnp.bfloat16),
            in_specs=[SMEM] + [VMEM] * 2 + [pl.BlockSpec(memory_space=pl.ANY)] * len(so_far),
            out_specs=VMEM,
            scratch_shapes=[
                pltpu.VMEM((chips * OWN * BLK, SEC * IBS * BLK), jnp.bfloat16),
                pltpu.VMEM((chips * OWN * BLK, NCC * BLK), jnp.bfloat16),
            ],
            input_output_aliases={3: 0} if so_far else {},
            cost_estimate=pl.CostEstimate(flops=10**9, bytes_accessed=4 * 10**6, transcendentals=0),
            compiler_params=pltpu.CompilerParams(vmem_limit_bytes=2 * SMALL),
        )(own, part_of_a, wide, *so_far)

    partial = products(1, a_other, products(0, a_own))

    def group(core, g):
        first = near * g + (near // 2) * core
        found = sorted(range(first, first + near), key=lambda z: z % near)
        return [core * layers + z % layers for z in found]

    close = [group(core, g) for core in range(CORES) for g in range(layers // near)]
    far = [[o + near * g for g in range(layers // near)] for o in range(near)]
    got = lax.all_to_all(partial, ("core", "layer"), 0, 0, axis_index_groups=close, tiled=True)
    part = got.astype(jnp.float32).sum(axis=0).astype(jnp.bfloat16)
    got = lax.all_to_all(part, "layer", 0, 0, axis_index_groups=far, tiled=True)
    return got.astype(jnp.float32).sum(axis=0).astype(jnp.bfloat16)[None, None]


def solution(mesh):
    rows, cols, layers = mesh.devices.shape
    split = jax.sharding.Mesh(
        mesh.devices.reshape(rows, cols // CORES, CORES, layers), ("row", "chip", "core", "layer")
    )
    col = ("chip", "core")
    return jax.shard_map(
        local,
        mesh=split,
        in_specs=(
            P("layer", None, ("row",) + col, None, None),
            P("layer", None, ("row",) + col, None),
            P("layer", None, col, "row", None, None),
            P("layer", None, col, "row", None),
            P(col, "row", None),
        ),
        out_specs=P(col, ("row", "layer"), None, None),
        check_vma=False,
    )
```

time: 227 us -> 113 us (0.50)
  the two profiles are of different devices: /device:TPU:2 before, /device:TPU:33 now
where the time goes in v1:
time: 113 us
  blocking collectives  77.8 us (69%)
  Pallas kernels  14.2 us (13%)
  starting transfers between devices  13.3 us (12%)
  waiting for transfers between devices  6.39 us (6%)
    all_to_all x1, blocking collectives, local(): lax.all_to_all(partial, ('core', 'layer'), 0, 0, axis_index_groups=close,...  31.5 us
    all_to_all x1, blocking collectives, local(): got = lax.all_to_all(part, 'layer', 0, 0, axis_index_groups=far, tiled=True)  27.3 us
    all_to_all x1, blocking collectives, local(): a_own = lax.all_to_all(a_out, 'chip', 0, 0, tiled=True)  19 us
    pallas_call x2, Pallas kernels, products(): pl.pallas_call(lambda *refs: product_kernel(near, side, *refs), out_shape...  9.6 us
    ppermute x3, starting transfers between devices, local(): lax.ppermute(p_out, 'row', [(i, (i + d) % rows) for i in range(rows)])  9.33 us
    ppermute x3, waiting for transfers between devices, local(): lax.ppermute(p_out, 'row', [(i, (i + d) % rows) for i in range(rows)])  6.39 us
    ppermute x1, starting transfers between devices, local(): a_other = lax.ppermute(a_own, 'core', [(0, 1), (1, 0)])  4 us
    pallas_call x1, Pallas kernels, local(): pl.pallas_call(expand_kernel, out_shape=jax.ShapeDtypeStruct((SEC * IBS *...  2.44 us
  transfers between devices with their start and end apart: 4, of which 2 were waited for; matrix products, arithmetic and copies ran while one was open for 0% of the time, Pallas kernels for 6%

profile of v1, /device:TPU:33, one launch (start us, length us, event | category | flops | bytes accessed | tf_op | source)
XLA Modules:
  0.0 112.9 jit_solution(8051135783365449102)
XLA Ops:
  0.0 2.1 %shard_map.55 = (bf16[4,272,512]{2,1,0:T(8,128)(2,1)}, bf16[272,256]{1,0:T(8,128)(2,1)}) custom-call(s32[1,2,2,8]{3,2,1,0:T(2,128)} %a_cols.1, s32[1,2,1,2,4]{4,3,2,1,0:T(2,128)} %p_cols.1, bf16[256,512]{1,0:T(8,128)(2,1)} %bitcast.5, bf16[256,256]{1,0:T(8,128)(2,1)} %bitcast.6), custom_call_target="tpu_custom_call" | custom-call | tf_op jit(solution)/shard_map/pallas_call | solution.py:140
  2.1 0.0 copy-start
  2.1 0.0 copy-start.1
  2.1 19.0 %all_to_all.15.refs_1_ = bf16[4,272,512]{2,1,0:T(8,128)(2,1)S(1)} all-to-all(bf16[4,272,512]{2,1,0:T(8,128)(2,1)} %get-tuple-element.7), channel_id=1, replica_groups=mesh['row'=4,'chip'=4,'core'=2,'layer'=16] {'chip'}, dimensions={0} | all-to-all | bytes 2228224 | tf_op jit(solution)/shard_map/all_to_all | solution.py:149
  21.1 4.0 %collective-permute-start = (bf16[4,272,512]{2,1,0:T(8,128)(2,1)S(1)}, bf16[4,272,512]{2,1,0:T(8,128)(2,1)S(1)}, u32[]{:S(2)}, u32[]{:S(2)}) collective-permute-start(bf16[4,272,512]{2,1,0:T(8,128)(2,1)S(1)} %all_to_all.15.refs_1_), channel_id=1, source_target_pairs={{0,16},{16,0},{1,17},{17,1},{2,18},{18,2},{3,19},{19,3},{4,20},{20... | collective-permute-start | bytes 3342344 | tf_op jit(solution)/shard_map/ppermute | solution.py:151
  25.1 0.0 copy-done
  25.1 4.4 %collective-permute-start.3 = (bf16[272,256]{1,0:T(8,128)(2,1)S(1)}, bf16[272,256]{1,0:T(8,128)(2,1)S(1)}, u32[]{:S(2)}, u32[]{:S(2)}) collective-permute-start(bf16[272,256]{1,0:T(8,128)(2,1)S(1)} %copy-done), channel_id=1, source_target_pairs={{0,384},{128,0},{256,128},{384,256},{1,385},{129,1},{257,129},{385... | collective-permute-start | bytes 417800 | tf_op jit(solution)/shard_map/ppermute | solution.py:150
  29.5 2.4 %collective-permute-start.2 = (bf16[272,256]{1,0:T(8,128)(2,1)S(1)}, bf16[272,256]{1,0:T(8,128)(2,1)S(1)}, u32[]{:S(2)}, u32[]{:S(2)}) collective-permute-start(bf16[272,256]{1,0:T(8,128)(2,1)S(1)} %copy-done), channel_id=1, source_target_pairs={{0,256},{128,384},{256,0},{384,128},{1,257},{129,385},{257,1},{385... | collective-permute-start | bytes 417800 | tf_op jit(solution)/shard_map/ppermute | solution.py:150
  31.9 2.5 %collective-permute-start.1 = (bf16[272,256]{1,0:T(8,128)(2,1)S(1)}, bf16[272,256]{1,0:T(8,128)(2,1)S(1)}, u32[]{:S(2)}, u32[]{:S(2)}) collective-permute-start(bf16[272,256]{1,0:T(8,128)(2,1)S(1)} %copy-done), channel_id=1, source_target_pairs={{0,128},{128,256},{256,384},{384,0},{1,129},{129,257},{257,385},{3... | collective-permute-start | bytes 417800 | tf_op jit(solution)/shard_map/ppermute | solution.py:150
  34.5 0.0 copy-done.1
  34.5 0.1 copy.9
  34.5 0.1 reshape.9
  34.6 0.1 pad_add_fusion.own.refs_0_
  34.7 0.0 collective-permute-done.3.refs_3_
  34.7 3.1 %collective-permute-done.2.refs_2_ = bf16[272,256]{1,0:T(8,128)(2,1)S(1)} collective-permute-done((bf16[272,256]{1,0:T(8,128)(2,1)S(1)}, bf16[272,256]{1,0:T(8,128)(2,1)S(1)}, u32[]{:S(2)}, u32[]{:S(2)}) %collective-permute-start.2) | collective-permute-done | bytes 139296 | tf_op jit(solution)/shard_map/ppermute | solution.py:150
  37.8 3.3 %collective-permute-done.1.refs_1_ = bf16[272,256]{1,0:T(8,128)(2,1)S(1)} collective-permute-done((bf16[272,256]{1,0:T(8,128)(2,1)S(1)}, bf16[272,256]{1,0:T(8,128)(2,1)S(1)}, u32[]{:S(2)}, u32[]{:S(2)}) %collective-permute-start.1) | collective-permute-done | bytes 139296 | tf_op jit(solution)/shard_map/ppermute | solution.py:150
  41.1 2.4 %shard_map.56.refs_2_ = bf16[1024,1024]{1,0:T(8,128)(2,1)S(1)} custom-call(s32[130]{0:T(256)S(1)} %pad_add_fusion.own.refs_0_, bf16[272,256]{1,0:T(8,128)(2,1)S(1)} %copy-done, bf16[272,256]{1,0:T(8,128)(2,1)S(1)} %collective-permute-done.1.refs_1_, bf16[272,256]{1,0:T(8,128)(2,1)S(1)} %collective-permute-done.2.refs_2_, ...), custom_call_target="tpu_custom_call" | custom-call | flops 1000000 | bytes 3000000 | tf_op jit(solution)/shard_map/pallas_call | solution.py:154
  43.5 4.8 %shard_map.57.refs_3_ = bf16[4,4,64,512]{3,2,1,0:T(8,128)(2,1)S(1)} custom-call(s32[130]{0:T(256)S(1)} %pad_add_fusion.own.refs_0_, bf16[4,272,512]{2,1,0:T(8,128)(2,1)S(1)} %all_to_all.15.refs_1_, bf16[1024,1024]{1,0:T(8,128)(2,1)S(1)} %shard_map.56.refs_2_), custom_call_target="tpu_custom_call" | custom-call | flops 1000000000 | bytes 4000000 | tf_op jit(solution)/shard_map/pallas_call | solution.py:164
  48.4 0.0 collective-permute-done.refs_1_
  48.4 4.8 %shard_map.58 = bf16[4,4,64,512]{3,2,1,0:T(8,128)(2,1)S(1)} custom-call(s32[130]{0:T(256)S(1)} %pad_add_fusion.own.refs_0_, bf16[4,272,512]{2,1,0:T(8,128)(2,1)S(1)} %collective-permute-done.refs_1_, bf16[1024,1024]{1,0:T(8,128)(2,1)S(1)} %shard_map.56.refs_2_, bf16[4,4,64,512]{3,2,1,0:T(8,128)(2,1)S(1)} %shard_map.57.refs_3_), custom_call_target="tpu_custom_call", output_to_operand_aliasing={{}: (3, {})} | custom-call | flops 1000000000 | bytes 4000000 | tf_op jit(solution)/shard_map/pallas_call | solution.py:164
  53.2 31.5 %all_to_all.16 = bf16[4,4,64,512]{3,2,1,0:T(8,128)(2,1)S(1)} all-to-all(bf16[4,4,64,512]{3,2,1,0:T(8,128)(2,1)S(1)} %shard_map.58), channel_id=1, replica_groups={{0,1,2,3},{4,5,6,7},{8,9,10,11},{12,13,14,15},{20,21,18,19},{24,25,22,2..., dimensions={0} | all-to-all | bytes 2097152 | tf_op jit(solution)/shard_map/all_to_all | solution.py:187
  84.7 0.2 reduce_sum.24
  84.9 27.3 %all_to_all.17 = bf16[4,64,512]{2,1,0:T(8,128)(2,1)S(1)} all-to-all(bf16[4,64,512]{2,1,0:T(8,128)(2,1)S(1)} %reduce_sum.24), channel_id=1, replica_groups={{0,4,8,12},{1,5,9,13},{2,6,10,14},{3,7,11,15},{16,20,24,28},{17,21,25,2..., dimensions={0} | all-to-all | bytes 524288 | tf_op jit(solution)/shard_map/all_to_all | solution.py:189
  112.2 0.7 reduce_sum.25
Async XLA Ops:
  2.1 23.0 %copy-start = (bf16[272,256]{1,0:T(8,128)(2,1)S(1)}, bf16[272,256]{1,0:T(8,128)(2,1)}, u32[]{:S(2)}) copy-start(bf16[272,256]{1,0:T(8,128)(2,1)} %get-tuple-element.8.refs_0_) | copy-start | bytes 417796
  2.1 32.3 %copy-start.1 = (s32[1,16,8]{1,2,0:T(8,128)S(1)}, s32[1,16,8]{1,2,0:T(8,128)}, u32[]{:S(2)}) copy-start(s32[1,16,8]{1,2,0:T(8,128)} %param.9) | copy-start | bytes 1540
  21.1 27.3 %collective-permute-start = (bf16[4,272,512]{2,1,0:T(8,128)(2,1)S(1)}, bf16[4,272,512]{2,1,0:T(8,128)(2,1)S(1)}, u32[]{:S(2)}, u32[]{:S(2)}) collective-permute-start(bf16[4,272,512]{2,1,0:T(8,128)(2,1)S(1)} %all_to_all.15.refs_1_), channel_id=1, source_target_pairs={{0,16},{16,0},{1,17},{17,1},{2,18},{18,2},{3,19},{19,3},{4,20},{20... | collective-permute-start | bytes 3342344 | tf_op jit(solution)/shard_map/ppermute | solution.py:151
  25.1 9.6 %collective-permute-start.3 = (bf16[272,256]{1,0:T(8,128)(2,1)S(1)}, bf16[272,256]{1,0:T(8,128)(2,1)S(1)}, u32[]{:S(2)}, u32[]{:S(2)}) collective-permute-start(bf16[272,256]{1,0:T(8,128)(2,1)S(1)} %copy-done), channel_id=1, source_target_pairs={{0,384},{128,0},{256,128},{384,256},{1,385},{129,1},{257,129},{385... | collective-permute-start | bytes 417800 | tf_op jit(solution)/shard_map/ppermute | solution.py:150
  29.5 8.3 %collective-permute-start.2 = (bf16[272,256]{1,0:T(8,128)(2,1)S(1)}, bf16[272,256]{1,0:T(8,128)(2,1)S(1)}, u32[]{:S(2)}, u32[]{:S(2)}) collective-permute-start(bf16[272,256]{1,0:T(8,128)(2,1)S(1)} %copy-done), channel_id=1, source_target_pairs={{0,256},{128,384},{256,0},{384,128},{1,257},{129,385},{257,1},{385... | collective-permute-start | bytes 417800 | tf_op jit(solution)/shard_map/ppermute | solution.py:150
  31.9 9.2 %collective-permute-start.1 = (bf16[272,256]{1,0:T(8,128)(2,1)S(1)}, bf16[272,256]{1,0:T(8,128)(2,1)S(1)}, u32[]{:S(2)}, u32[]{:S(2)}) collective-permute-start(bf16[272,256]{1,0:T(8,128)(2,1)S(1)} %copy-done), channel_id=1, source_target_pairs={{0,128},{128,256},{256,384},{384,0},{1,129},{129,257},{257,385},{3... | collective-permute-start | bytes 417800 | tf_op jit(solution)/shard_map/ppermute | solution.py:150

commit v2 on v1

--- a/solution.py
+++ b/solution.py
@@ -22,6 +22,7 @@
 STEP = 16
 VMEM = pl.BlockSpec(memory_space=pltpu.VMEM)
 SMEM = pl.BlockSpec(memory_space=pltpu.SMEM)
+HBM = pl.BlockSpec(memory_space=pltpu.HBM)
 
 
 def repeat(count, unroll, step):
@@ -41,16 +42,24 @@
     return row.astype(jnp.bfloat16)
 
 
-def pack_kernel(a_cols, p_cols, a_blocks, p_blocks, a_out, p_out):
+def pack_kernel(a_cols_hbm, p_cols_hbm, a_blocks, p_blocks, a_out, p_out, a_cols, p_cols, sems):
+    places = [a_out.at[n, :BODY] for n in range(a_out.shape[0])]
+    moves = [(a_cols_hbm, a_cols), (p_cols_hbm, p_cols), (p_blocks, p_out.at[:BODY])]
+    moves += [(a_blocks, place) for place in places]
+    copies = [pltpu.make_async_copy(src, dst, sems.at[n]) for n, (src, dst) in enumerate(moves)]
+    for copy in copies:
+        copy.start()
+    copies[0].wait()
+    copies[1].wait()
     a_head = head_row([a_cols[0, s, j, k] for s in range(SEC) for j in range(OWN) for k in range(KS)])
     p_head = head_row([p_cols[0, s, 0, j, q] for s in range(SEC) for j in range(OWN) for q in range(KP)])
     for n in range(a_out.shape[0]):
-        a_out[n, :BODY, :] = a_blocks[...]
         a_out[n, BODY:, :] = jnp.zeros((HEAD, KS * BLK), jnp.bfloat16)
         a_out[n, BODY:, :PAIR] = a_head
-    p_out[:BODY, :] = p_blocks[...]
     p_out[BODY:, :] = jnp.zeros((HEAD, KP * BLK), jnp.bfloat16)
     p_out[BODY:, :PAIR] = p_head
+    for copy in copies[2:]:
+        copy.wait()
 
 
 def twins(two):
@@ -76,10 +85,16 @@
     return [[place + 2 * pair == col for col in cols] for pair in range(pairs)]
 
 
-def expand_kernel(own, *refs):
-    p_parts, wide = refs[:-1], refs[-1]
-    for d, p_ref in enumerate(p_parts):
-        src = lax.rem(own[1] - d + len(p_parts), len(p_parts))
+def expand_kernel(*refs):
+    held, sems = refs[-2:]
+    p_parts, wide = refs[:-3], refs[-3]
+    copies = [pltpu.make_async_copy(part, held.at[d], sems.at[d]) for d, part in enumerate(p_parts)]
+    for copy in copies:
+        copy.start()
+    for d, copy in enumerate(copies):
+        copy.wait()
+        p_ref = held.at[d]
+        src = lax.rem(lax.axis_index("row") - d + len(p_parts), len(p_parts))
         head = p_ref[BODY:, :PAIR].astype(jnp.float32)
         for n in range(SEC * OWN):
             s, j = n // OWN, n % OWN
@@ -94,11 +109,11 @@
                     wide[pl.ds(slab + g * STEP, STEP), pair * PAIR : (pair + 1) * PAIR] = acc.astype(jnp.bfloat16)
 
 
-def product_kernel(near, side, own, a_ref, wide, *refs):
+def product_kernel(near, side, c_cols, a_ref, wide, *refs):
     out, rows, full = refs[-3:]
-    owner = own[0] if side == 0 else 1 - own[0]
+    core = lax.axis_index("core")
+    owner = core if side == 0 else 1 - core
     parts = a_ref.shape[0]
-    c_at = 2
 
     def gather(src):
         head = a_ref[src, BODY:, :PAIR].astype(jnp.float32)
@@ -126,7 +141,7 @@
         for pair in range(KC // 2):
             picked = []
             for m in range(2):
-                c = own[c_at + i * KC + pair * 2 + m]
+                c = c_cols[0, pair * 2 + m, i]
                 two = full[pl.ds(row, BLK), pl.ds(pl.multiple_of(c // 2 * PAIR, PAIR), PAIR)]
                 picked.append(jnp.where(lax.rem(c, 2) == m, two, swap(two)))
             out[lax.rem(i, near), i // near, :, pair * PAIR : (pair + 1) * PAIR] = jnp.where(low, *picked)
@@ -143,22 +158,29 @@
             jax.ShapeDtypeStruct((chips, BODY + HEAD, KS * BLK), jnp.bfloat16),
             jax.ShapeDtypeStruct((BODY + HEAD, KP * BLK), jnp.bfloat16),
         ),
-        in_specs=[SMEM, SMEM, VMEM, VMEM],
+        in_specs=[HBM] * 4,
         out_specs=(VMEM, VMEM),
+        scratch_shapes=[
+            pltpu.SMEM(a_cols.shape, jnp.int32),
+            pltpu.SMEM(p_cols.shape, jnp.int32),
+            pltpu.SemaphoreType.DMA((chips + 3,)),
+        ],
     )(a_cols, p_cols, a_blocks.reshape(BODY, KS * BLK), p_blocks.reshape(BODY, KP * BLK))
     a_own = lax.all_to_all(a_out, "chip", 0, 0, tiled=True)
     p_parts = [p_out] + [lax.ppermute(p_out, "row", [(i, (i + d) % rows) for i in range(rows)]) for d in range(1, rows)]
     a_other = lax.ppermute(a_own, "core", [(0, 1), (1, 0)])
-    own = jnp.stack([lax.axis_index("core"), lax.axis_index("row")]).astype(jnp.int32)
-    own = jnp.concatenate([own, c_cols.reshape(-1)])
     wide = pl.pallas_call(
         expand_kernel,
         out_shape=jax.ShapeDtypeStruct((SEC * IBS * BLK, NCC * BLK), jnp.bfloat16),
-        in_specs=[SMEM] + [VMEM] * rows,
+        in_specs=[HBM] * rows,
         out_specs=VMEM,
+        scratch_shapes=[
+            pltpu.VMEM((rows, BODY + HEAD, KP * BLK), jnp.bfloat16),
+            pltpu.SemaphoreType.DMA((rows,)),
+        ],
         cost_estimate=pl.CostEstimate(flops=10**6, bytes_accessed=3 * 10**6, transcendentals=0),
         compiler_params=pltpu.CompilerParams(vmem_limit_bytes=SMALL),
-    )(own, *p_parts)
+    )(*p_parts)
 
     def products(side, part_of_a, *so_far):
         return pl.pallas_call(
@@ -173,7 +195,7 @@
             input_output_aliases={3: 0} if so_far else {},
             cost_estimate=pl.CostEstimate(flops=10**9, bytes_accessed=4 * 10**6, transcendentals=0),
             compiler_params=pltpu.CompilerParams(vmem_limit_bytes=2 * SMALL),
-        )(own, part_of_a, wide, *so_far)
+        )(c_cols.transpose(0, 2, 1), part_of_a, wide, *so_far)
 
     partial = products(1, a_other, products(0, a_own))
 

time: 113 us -> 114 us (level)
  transfers between devices with their start and end apart: 4 -> 4, of which waited for: 2 -> 2; matrix products, arithmetic and copies ran while one was open for 0% -> 0% of each run, Pallas kernels for 6% -> 7%
where the time goes in v2:
time: 114 us
  blocking collectives  77.8 us (68%)
  Pallas kernels  15 us (13%)
  starting transfers between devices  13.3 us (12%)
  waiting for transfers between devices  6.64 us (6%)
    all_to_all x1, blocking collectives, local(): lax.all_to_all(partial, ('core', 'layer'), 0, 0, axis_index_groups=close,...  31.5 us
    all_to_all x1, blocking collectives, local(): got = lax.all_to_all(part, 'layer', 0, 0, axis_index_groups=far, tiled=True)  27.3 us
    all_to_all x1, blocking collectives, local(): a_own = lax.all_to_all(a_out, 'chip', 0, 0, tiled=True)  19 us
    pallas_call x2, Pallas kernels, products(): pl.pallas_call(lambda *refs: product_kernel(near, side, *refs), out_shape...  9.74 us
    ppermute x3, starting transfers between devices, local(): lax.ppermute(p_out, 'row', [(i, (i + d) % rows) for i in range(rows)])  9.33 us
    ppermute x3, waiting for transfers between devices, local(): lax.ppermute(p_out, 'row', [(i, (i + d) % rows) for i in range(rows)])  6.64 us
    ppermute x1, starting transfers between devices, local(): a_other = lax.ppermute(a_own, 'core', [(0, 1), (1, 0)])  4 us
    pallas_call x1, Pallas kernels, local(): pl.pallas_call(expand_kernel, out_shape=jax.ShapeDtypeStruct((SEC * IBS *...  2.66 us
  transfers between devices with their start and end apart: 4, of which 2 were waited for; matrix products, arithmetic and copies ran while one was open for 0% of the time, Pallas kernels for 7%

profile of v2, /device:TPU:33, one launch (start us, length us, event | category | flops | bytes accessed | tf_op | source)
XLA Modules:
  0.0 113.7 jit_solution(7059765528032694859)
XLA Ops:
  0.0 2.5 %shard_map.55 = (bf16[4,272,512]{2,1,0:T(8,128)(2,1)}, bf16[272,256]{1,0:T(8,128)(2,1)}) custom-call(s32[1,2,2,8]{3,2,1,0:T(2,128)} %a_cols_hbm.1, s32[1,2,1,2,4]{4,3,2,1,0:T(2,128)} %p_cols_hbm.1, bf16[256,512]{1,0:T(8,128)(2,1)} %bitcast.6, bf16[256,256]{1,0:T(8,128)(2,1)} %bitcast.7), custom_call_target="tpu_custom_call" | custom-call | tf_op jit(solution)/shard_map/pallas_call | solution.py:155
  2.6 0.0 copy-start
  2.6 19.0 %all_to_all.15.refs_1_ = bf16[4,272,512]{2,1,0:T(8,128)(2,1)S(1)} all-to-all(bf16[4,272,512]{2,1,0:T(8,128)(2,1)} %get-tuple-element.7), channel_id=1, replica_groups=mesh['row'=4,'chip'=4,'core'=2,'layer'=16] {'chip'}, dimensions={0} | all-to-all | bytes 2228224 | tf_op jit(solution)/shard_map/all_to_all | solution.py:169
  21.5 4.0 %collective-permute-start = (bf16[4,272,512]{2,1,0:T(8,128)(2,1)S(1)}, bf16[4,272,512]{2,1,0:T(8,128)(2,1)S(1)}, u32[]{:S(2)}, u32[]{:S(2)}) collective-permute-start(bf16[4,272,512]{2,1,0:T(8,128)(2,1)S(1)} %all_to_all.15.refs_1_), channel_id=1, source_target_pairs={{0,16},{16,0},{1,17},{17,1},{2,18},{18,2},{3,19},{19,3},{4,20},{20... | collective-permute-start | bytes 3342344 | tf_op jit(solution)/shard_map/ppermute | solution.py:171
  25.5 0.0 copy-done
  25.6 0.0 copy-start.1
  25.6 4.4 %collective-permute-start.3 = (bf16[272,256]{1,0:T(8,128)(2,1)S(1)}, bf16[272,256]{1,0:T(8,128)(2,1)S(1)}, u32[]{:S(2)}, u32[]{:S(2)}) collective-permute-start(bf16[272,256]{1,0:T(8,128)(2,1)S(1)} %copy-done), channel_id=1, source_target_pairs={{0,384},{128,0},{256,128},{384,256},{1,385},{129,1},{257,129},{385... | collective-permute-start | bytes 417800 | tf_op jit(solution)/shard_map/ppermute | solution.py:170
  30.0 2.4 %collective-permute-start.2 = (bf16[272,256]{1,0:T(8,128)(2,1)S(1)}, bf16[272,256]{1,0:T(8,128)(2,1)S(1)}, u32[]{:S(2)}, u32[]{:S(2)}) collective-permute-start(bf16[272,256]{1,0:T(8,128)(2,1)S(1)} %copy-done), channel_id=1, source_target_pairs={{0,256},{128,384},{256,0},{384,128},{1,257},{129,385},{257,1},{385... | collective-permute-start | bytes 417800 | tf_op jit(solution)/shard_map/ppermute | solution.py:170
  32.4 2.5 %collective-permute-start.1 = (bf16[272,256]{1,0:T(8,128)(2,1)S(1)}, bf16[272,256]{1,0:T(8,128)(2,1)S(1)}, u32[]{:S(2)}, u32[]{:S(2)}) collective-permute-start(bf16[272,256]{1,0:T(8,128)(2,1)S(1)} %copy-done), channel_id=1, source_target_pairs={{0,128},{128,256},{256,384},{384,0},{1,129},{129,257},{257,385},{3... | collective-permute-start | bytes 417800 | tf_op jit(solution)/shard_map/ppermute | solution.py:170
  34.9 0.0 collective-permute-done.3.refs_3_
  34.9 3.4 %collective-permute-done.2.refs_2_ = bf16[272,256]{1,0:T(8,128)(2,1)S(1)} collective-permute-done((bf16[272,256]{1,0:T(8,128)(2,1)S(1)}, bf16[272,256]{1,0:T(8,128)(2,1)S(1)}, u32[]{:S(2)}, u32[]{:S(2)}) %collective-permute-start.2) | collective-permute-done | bytes 139296 | tf_op jit(solution)/shard_map/ppermute | solution.py:170
  38.3 3.3 %collective-permute-done.1.refs_1_ = bf16[272,256]{1,0:T(8,128)(2,1)S(1)} collective-permute-done((bf16[272,256]{1,0:T(8,128)(2,1)S(1)}, bf16[272,256]{1,0:T(8,128)(2,1)S(1)}, u32[]{:S(2)}, u32[]{:S(2)}) %collective-permute-start.1) | collective-permute-done | bytes 139296 | tf_op jit(solution)/shard_map/ppermute | solution.py:170
  41.6 2.7 %shard_map.56.refs_2_ = bf16[1024,1024]{1,0:T(8,128)(2,1)S(1)} custom-call(bf16[272,256]{1,0:T(8,128)(2,1)S(1)} %copy-done, bf16[272,256]{1,0:T(8,128)(2,1)S(1)} %collective-permute-done.1.refs_1_, bf16[272,256]{1,0:T(8,128)(2,1)S(1)} %collective-permute-done.2.refs_2_, bf16[272,256]{1,0:T(8,128)(2,1)S(1)} %collective-permute-done.3.refs_3_), custom_call_target="tpu_custom_call" | custom-call | flops 1000000 | bytes 3000000 | tf_op jit(solution)/shard_map/pallas_call | solution.py:172
  44.2 0.0 copy-done.1
  44.3 4.9 %shard_map.57.refs_3_ = bf16[4,4,64,512]{3,2,1,0:T(8,128)(2,1)S(1)} custom-call(s32[1,8,16]{2,1,0:T(8,128)S(1)} %bitcast.4, bf16[4,272,512]{2,1,0:T(8,128)(2,1)S(1)} %all_to_all.15.refs_1_, bf16[1024,1024]{1,0:T(8,128)(2,1)S(1)} %shard_map.56.refs_2_), custom_call_target="tpu_custom_call" | custom-call | flops 1000000000 | bytes 4000000 | tf_op jit(solution)/shard_map/pallas_call | solution.py:186
  49.1 0.0 collective-permute-done.refs_1_
  49.1 4.9 %shard_map.58 = bf16[4,4,64,512]{3,2,1,0:T(8,128)(2,1)S(1)} custom-call(s32[1,8,16]{2,1,0:T(8,128)S(1)} %bitcast.5, bf16[4,272,512]{2,1,0:T(8,128)(2,1)S(1)} %collective-permute-done.refs_1_, bf16[1024,1024]{1,0:T(8,128)(2,1)S(1)} %shard_map.56.refs_2_, bf16[4,4,64,512]{3,2,1,0:T(8,128)(2,1)S(1)} %shard_map.57.refs_3_), custom_call_target="tpu_custom_call", output_to_operand_aliasing={{}: (3, {})} | custom-call | flops 1000000000 | bytes 4000000 | tf_op jit(solution)/shard_map/pallas_call | solution.py:186
  54.0 31.5 %all_to_all.16 = bf16[4,4,64,512]{3,2,1,0:T(8,128)(2,1)S(1)} all-to-all(bf16[4,4,64,512]{3,2,1,0:T(8,128)(2,1)S(1)} %shard_map.58), channel_id=1, replica_groups={{0,1,2,3},{4,5,6,7},{8,9,10,11},{12,13,14,15},{20,21,18,19},{24,25,22,2..., dimensions={0} | all-to-all | bytes 2097152 | tf_op jit(solution)/shard_map/all_to_all | solution.py:209
  85.5 0.2 reduce_sum.24
  85.7 27.3 %all_to_all.17 = bf16[4,64,512]{2,1,0:T(8,128)(2,1)S(1)} all-to-all(bf16[4,64,512]{2,1,0:T(8,128)(2,1)S(1)} %reduce_sum.24), channel_id=1, replica_groups={{0,4,8,12},{1,5,9,13},{2,6,10,14},{3,7,11,15},{16,20,24,28},{17,21,25,2..., dimensions={0} | all-to-all | bytes 524288 | tf_op jit(solution)/shard_map/all_to_all | solution.py:211
  113.0 0.7 reduce_sum.25
Async XLA Ops:
  2.6 23.0 %copy-start = (bf16[272,256]{1,0:T(8,128)(2,1)S(1)}, bf16[272,256]{1,0:T(8,128)(2,1)}, u32[]{:S(2)}) copy-start(bf16[272,256]{1,0:T(8,128)(2,1)} %get-tuple-element.8.refs_0_) | copy-start | bytes 417796
  21.5 27.6 %collective-permute-start = (bf16[4,272,512]{2,1,0:T(8,128)(2,1)S(1)}, bf16[4,272,512]{2,1,0:T(8,128)(2,1)S(1)}, u32[]{:S(2)}, u32[]{:S(2)}) collective-permute-start(bf16[4,272,512]{2,1,0:T(8,128)(2,1)S(1)} %all_to_all.15.refs_1_), channel_id=1, source_target_pairs={{0,16},{16,0},{1,17},{17,1},{2,18},{18,2},{3,19},{19,3},{4,20},{20... | collective-permute-start | bytes 3342344 | tf_op jit(solution)/shard_map/ppermute | solution.py:171
  25.6 18.7 %copy-start.1 = (s32[1,16,8]{1,2,0:T(8,128)S(1)}, s32[1,16,8]{1,2,0:T(8,128)}, u32[]{:S(2)}) copy-start(s32[1,16,8]{1,2,0:T(8,128)} %param.9) | copy-start | bytes 1540
  25.6 9.4 %collective-permute-start.3 = (bf16[272,256]{1,0:T(8,128)(2,1)S(1)}, bf16[272,256]{1,0:T(8,128)(2,1)S(1)}, u32[]{:S(2)}, u32[]{:S(2)}) collective-permute-start(bf16[272,256]{1,0:T(8,128)(2,1)S(1)} %copy-done), channel_id=1, source_target_pairs={{0,384},{128,0},{256,128},{384,256},{1,385},{129,1},{257,129},{385... | collective-permute-start | bytes 417800 | tf_op jit(solution)/shard_map/ppermute | solution.py:170
  30.0 8.3 %collective-permute-start.2 = (bf16[272,256]{1,0:T(8,128)(2,1)S(1)}, bf16[272,256]{1,0:T(8,128)(2,1)S(1)}, u32[]{:S(2)}, u32[]{:S(2)}) collective-permute-start(bf16[272,256]{1,0:T(8,128)(2,1)S(1)} %copy-done), channel_id=1, source_target_pairs={{0,256},{128,384},{256,0},{384,128},{1,257},{129,385},{257,1},{385... | collective-permute-start | bytes 417800 | tf_op jit(solution)/shard_map/ppermute | solution.py:170
  32.4 9.2 %collective-permute-start.1 = (bf16[272,256]{1,0:T(8,128)(2,1)S(1)}, bf16[272,256]{1,0:T(8,128)(2,1)S(1)}, u32[]{:S(2)}, u32[]{:S(2)}) collective-permute-start(bf16[272,256]{1,0:T(8,128)(2,1)S(1)} %copy-done), channel_id=1, source_target_pairs={{0,128},{128,256},{256,384},{384,0},{1,129},{129,257},{257,385},{3... | collective-permute-start | bytes 417800 | tf_op jit(solution)/shard_map/ppermute | solution.py:170

commit v3 on v1

v3 whole, which is shorter than its diff:
```python
import jax
import jax.numpy as jnp
from jax import lax
from jax.experimental import pallas as pl
from jax.experimental.pallas import tpu as pltpu
from jax.sharding import PartitionSpec as P


BLK = 64
KS = 8
KP = 4
KC = 8
NCC = 16
SEC = 2
OWN = 2
IBS = 8
CORES = 2
HEAD = 16
BODY = SEC * OWN * BLK
PAIR = 2 * BLK
SMALL = 8 * 1024 * 1024
SHIFTS = ((0, 3), (2, 1))
HALF = 2
STEP = 16
VMEM = pl.BlockSpec(memory_space=pltpu.VMEM)
SMEM = pl.BlockSpec(memory_space=pltpu.SMEM)
HBM = pl.BlockSpec(memory_space=pltpu.HBM)


def repeat(count, unroll, step):
    def several(t, _):
        for u in range(unroll):
            step(t * unroll + u)
        return 0

    lax.fori_loop(0, count // unroll, several, 0)


def head_row(values):
    lane = lax.broadcasted_iota(jnp.int32, (HEAD, PAIR), 1)
    row = jnp.zeros((HEAD, PAIR), jnp.float32)
    for n, value in enumerate(values):
        row = jnp.where(lane == n, value.astype(jnp.float32), row)
    return row.astype(jnp.bfloat16)


def pack_kernel(a_cols, p_cols, a_blocks, p_blocks, a_out, p_out):
    a_head = head_row([a_cols[0, s, j, k] for s in range(SEC) for j in range(OWN) for k in range(KS)])
    p_head = head_row([p_cols[0, s, 0, j, q] for s in range(SEC) for j in range(OWN) for q in range(KP)])
    for n in range(a_out.shape[0]):
        a_out[n, :BODY, :] = a_blocks[...]
        a_out[n, BODY:, :] = jnp.zeros((HEAD, KS * BLK), jnp.bfloat16)
        a_out[n, BODY:, :PAIR] = a_head
    p_out[:BODY, :] = p_blocks[...]
    p_out[BODY:, :] = jnp.zeros((HEAD, KP * BLK), jnp.bfloat16)
    p_out[BODY:, :PAIR] = p_head


def twins(two):
    turned = pltpu.roll(two, BLK, 1)
    low = lax.broadcasted_iota(jnp.int32, two.shape, 1) < BLK
    return jnp.where(low, two, turned), jnp.where(low, turned, two)


def copies_of(tile):
    found = []
    for t in range(tile.shape[1] // PAIR):
        found.extend(twins(tile[:, t * PAIR : (t + 1) * PAIR].astype(jnp.float32)))
    return found


def swap(tile):
    return jnp.concatenate([tile[:, BLK:], tile[:, :BLK]], axis=1)


def masks_of(head, first, count, pairs):
    half = lax.broadcasted_iota(jnp.int32, (STEP, PAIR), 1) // BLK
    cols = [jnp.broadcast_to(head[:, first + n : first + n + 1], (STEP, PAIR)) for n in range(count)]
    return [[(half + 2 * pair).astype(jnp.float32) == col for col in cols] for pair in pairs]


def source_of(shift, axis):
    size = lax.axis_size(axis)
    return lax.rem(lax.axis_index(axis) - shift + size, size)


def expand_kernel(*refs):
    p_parts, (wide, held, sems) = refs[:HALF], refs[HALF:]
    copies = [pltpu.make_async_copy(part, held.at[n], sems.at[n]) for n, part in enumerate(p_parts)]
    for copy in copies:
        copy.start()
    for place, copy in enumerate(copies):
        copy.wait()
        head = held[place, BODY:, :PAIR].astype(jnp.float32)
        for n in range(SEC * OWN):
            s, j = n // OWN, n % OWN
            masks = masks_of(head, n * KP, KP, range(NCC // 2))
            slab = ((s * HALF + place) * OWN + j) * BLK
            for g in range(BLK // STEP):
                copies_in = copies_of(held[place, n * BLK + g * STEP : n * BLK + (g + 1) * STEP, :])
                for pair in range(NCC // 2):
                    acc = jnp.where(masks[pair][0], copies_in[0], 0.0)
                    for q in range(1, KP):
                        acc = jnp.where(masks[pair][q], copies_in[q], acc)
                    first = slab + g * STEP
                    wide[first : first + STEP, pair * PAIR : (pair + 1) * PAIR] = acc.astype(jnp.bfloat16)


def product_kernel(near, c_cols, a_own, a_other, wide_first, wide_second, out, rows, full):
    core = lax.axis_index("core")
    parts = a_own.shape[0]
    sources = [[source_of(shift, "row") for shift in shifts] for shifts in SHIFTS]
    for side, a_ref in enumerate((a_own, a_other)):

        def gather(src, side=side, a_ref=a_ref):
            head = a_ref[src, BODY:, :PAIR].astype(jnp.float32)
            for j in range(OWN):
                row = pl.multiple_of(((side * parts + src) * OWN + j) * BLK, BLK)
                for s in range(SEC):
                    masks = masks_of(head, (s * OWN + j) * KS, KS, sources[0] + sources[1])
                    for g in range(BLK // STEP):
                        first = (s * OWN + j) * BLK + g * STEP
                        copies = copies_of(a_ref[src, first : first + STEP, :])
                        for pair in range(IBS // OWN):
                            acc = jnp.where(masks[pair][0], copies[0], 0.0)
                            for k in range(1, KS):
                                acc = acc + jnp.where(masks[pair][k], copies[k], 0.0)
                            lane = ((pair // HALF * SEC + s) * HALF + pair % HALF) * PAIR
                            rows[pl.ds(row + g * STEP, STEP), lane : lane + PAIR] = acc.astype(jnp.bfloat16)

        repeat(parts, 2, gather)

    wide = jnp.concatenate([wide_first[...], wide_second[...]], axis=0)
    full[...] = jnp.dot(rows[...], wide, preferred_element_type=jnp.float32).astype(jnp.bfloat16)
    low = lax.broadcasted_iota(jnp.int32, (BLK, PAIR), 1).astype(jnp.int16) < jnp.int16(BLK)
    for side in range(CORES):
        owner = core if side == 0 else 1 - core

        def pick(n, side=side, owner=owner):
            i = (n // OWN * CORES + owner) * OWN + lax.rem(n, OWN)
            row = pl.multiple_of((side * parts * OWN + n) * BLK, BLK)
            for pair in range(KC // 2):
                picked = []
                for m in range(2):
                    c = c_cols[0, pair * 2 + m, i]
                    two = full[pl.ds(row, BLK), pl.ds(pl.multiple_of(c // 2 * PAIR, PAIR), PAIR)]
                    picked.append(jnp.where(lax.rem(c, 2) == m, two, swap(two)))
                out[lax.rem(i, near), i // near, :, pair * PAIR : (pair + 1) * PAIR] = jnp.where(low, *picked)

        repeat(parts * OWN, 8, pick)


def local(a_blocks, a_cols, p_blocks, p_cols, c_cols):
    rows, chips, layers = lax.axis_size("row"), lax.axis_size("chip"), lax.axis_size("layer")
    near = 4
    a_out, p_out = pl.pallas_call(
        pack_kernel,
        out_shape=(
            jax.ShapeDtypeStruct((chips, BODY + HEAD, KS * BLK), jnp.bfloat16),
            jax.ShapeDtypeStruct((BODY + HEAD, KP * BLK), jnp.bfloat16),
        ),
        in_specs=[SMEM, SMEM, VMEM, VMEM],
        out_specs=(VMEM, VMEM),
    )(a_cols, p_cols, a_blocks.reshape(BODY, KS * BLK), p_blocks.reshape(BODY, KP * BLK))

    def expand(*parts):
        return pl.pallas_call(
            expand_kernel,
            out_shape=jax.ShapeDtypeStruct((HALF * SEC * OWN * BLK, NCC * BLK), jnp.bfloat16),
            in_specs=[HBM] * HALF,
            out_specs=VMEM,
            scratch_shapes=[
                pltpu.VMEM((HALF, BODY + HEAD, KP * BLK), jnp.bfloat16),
                pltpu.SemaphoreType.DMA((HALF,)),
            ],
            cost_estimate=pl.CostEstimate(flops=10**6, bytes_accessed=2 * 10**6, transcendentals=0),
            compiler_params=pltpu.CompilerParams(vmem_limit_bytes=SMALL),
        )(*parts)

    a_own = lax.all_to_all(a_out, "chip", 0, 0, tiled=True)
    p_parts = [p_out] + [lax.ppermute(p_out, "row", [(i, (i + d) % rows) for i in range(rows)]) for d in range(1, rows)]
    first = expand(*[p_parts[d] for d in SHIFTS[0]])
    a_other = lax.ppermute(a_own, "core", [(0, 1), (1, 0)])
    second = expand(*[p_parts[d] for d in SHIFTS[1]])
    partial = pl.pallas_call(
        lambda *refs: product_kernel(near, *refs),
        out_shape=jax.ShapeDtypeStruct((near, layers // near, BLK, KC * BLK), jnp.bfloat16),
        in_specs=[SMEM] + [VMEM] * 4,
        out_specs=VMEM,
        scratch_shapes=[
            pltpu.VMEM((chips * CORES * OWN * BLK, SEC * IBS * BLK), jnp.bfloat16),
            pltpu.VMEM((chips * CORES * OWN * BLK, NCC * BLK), jnp.bfloat16),
        ],
        cost_estimate=pl.CostEstimate(flops=2 * 10**9, bytes_accessed=4 * 10**6, transcendentals=0),
        compiler_params=pltpu.CompilerParams(vmem_limit_bytes=3 * SMALL),
    )(c_cols.transpose(0, 2, 1), a_own, a_other, first, second)

    def group(core, g):
        first = near * g + (near // 2) * core
        found = sorted(range(first, first + near), key=lambda z: z % near)
        return [core * layers + z % layers for z in found]

    close = [group(core, g) for core in range(CORES) for g in range(layers // near)]
    far = [[o + near * g for g in range(layers // near)] for o in range(near)]
    got = lax.all_to_all(partial, ("core", "layer"), 0, 0, axis_index_groups=close, tiled=True)
    part = got.astype(jnp.float32).sum(axis=0).astype(jnp.bfloat16)
    got = lax.all_to_all(part, "layer", 0, 0, axis_index_groups=far, tiled=True)
    return got.astype(jnp.float32).sum(axis=0).astype(jnp.bfloat16)[None, None]


def solution(mesh):
    rows, cols, layers = mesh.devices.shape
    split = jax.sharding.Mesh(
        mesh.devices.reshape(rows, cols // CORES, CORES, layers), ("row", "chip", "core", "layer")
    )
    col = ("chip", "core")
    return jax.shard_map(
        local,
        mesh=split,
        in_specs=(
            P("layer", None, ("row",) + col, None, None),
            P("layer", None, ("row",) + col, None),
            P("layer", None, col, "row", None, None),
            P("layer", None, col, "row", None),
            P(col, "row", None),
        ),
        out_specs=P(col, ("row", "layer"), None, None),
        check_vma=False,
    )
```

time: 113 us -> 109 us (0.965)
  waiting for transfers between devices: 6.39 us -> 3.56 us
  Pallas kernels: 14.2 us -> 12.8 us
    ppermute x3, waiting for transfers between devices: 6.39 us -> 3.56 us  [local(): lax.ppermute(p_out, 'row', [(i, (i + d) % rows) for i in range(rows)])]
    pallas_call x3, Pallas kernels: 12 us -> 10.7 us  [the longest x1 8.35 us: local(): pl.pallas_call(lambda *refs: product_kernel(near, *refs), out_shape=jax.S...]
  transfers between devices with their start and end apart: 4 -> 4, of which waited for: 2 -> 2; matrix products, arithmetic and copies ran while one was open for 0% -> 0% of each run, Pallas kernels for 6% -> 2%
where the time goes in v3:
time: 109 us
  blocking collectives  77.8 us (71%)
  starting transfers between devices  13.9 us (13%)
  Pallas kernels  12.8 us (12%)
  waiting for transfers between devices  3.56 us (3%)
    all_to_all x1, blocking collectives, local(): lax.all_to_all(partial, ('core', 'layer'), 0, 0, axis_index_groups=close,...  31.5 us
    all_to_all x1, blocking collectives, local(): got = lax.all_to_all(part, 'layer', 0, 0, axis_index_groups=far, tiled=True)  27.3 us
    all_to_all x1, blocking collectives, local(): a_own = lax.all_to_all(a_out, 'chip', 0, 0, tiled=True)  19 us
    ppermute x3, starting transfers between devices, local(): lax.ppermute(p_out, 'row', [(i, (i + d) % rows) for i in range(rows)])  9.93 us
    pallas_call x1, Pallas kernels, local(): pl.pallas_call(lambda *refs: product_kernel(near, *refs), out_shape=jax.S...  8.35 us
    ppermute x1, starting transfers between devices, local(): a_other = lax.ppermute(a_own, 'core', [(0, 1), (1, 0)])  4 us
    ppermute x3, waiting for transfers between devices, local(): lax.ppermute(p_out, 'row', [(i, (i + d) % rows) for i in range(rows)])  3.56 us
    pallas_call x2, Pallas kernels, expand(): pl.pallas_call(expand_kernel, out_shape=jax.ShapeDtypeStruct((HALF * SEC...  2.32 us
  transfers between devices with their start and end apart: 4, of which 2 were waited for; matrix products, arithmetic and copies ran while one was open for 0% of the time, Pallas kernels for 2%

profile of v3, /device:TPU:33, one launch (start us, length us, event | category | flops | bytes accessed | tf_op | source)
XLA Modules:
  0.0 109.1 jit_solution(12838011932376604596)
XLA Ops:
  0.0 2.1 %shard_map.55 = (bf16[4,272,512]{2,1,0:T(8,128)(2,1)}, bf16[272,256]{1,0:T(8,128)(2,1)}) custom-call(s32[1,2,2,8]{3,2,1,0:T(2,128)} %a_cols.1, s32[1,2,1,2,4]{4,3,2,1,0:T(2,128)} %p_cols.1, bf16[256,512]{1,0:T(8,128)(2,1)} %bitcast.5, bf16[256,256]{1,0:T(8,128)(2,1)} %bitcast.6), custom_call_target="tpu_custom_call" | custom-call | tf_op jit(solution)/shard_map/pallas_call | solution.py:156
  2.1 0.0 copy-start
  2.1 19.0 %all_to_all.15.refs_1_ = bf16[4,272,512]{2,1,0:T(8,128)(2,1)S(1)} all-to-all(bf16[4,272,512]{2,1,0:T(8,128)(2,1)} %get-tuple-element.7), channel_id=1, replica_groups=mesh['row'=4,'chip'=4,'core'=2,'layer'=16] {'chip'}, dimensions={0} | all-to-all | bytes 2228224 | tf_op jit(solution)/shard_map/all_to_all | solution.py:180
  21.1 4.0 %collective-permute-start = (bf16[4,272,512]{2,1,0:T(8,128)(2,1)S(1)}, bf16[4,272,512]{2,1,0:T(8,128)(2,1)S(1)}, u32[]{:S(2)}, u32[]{:S(2)}) collective-permute-start(bf16[4,272,512]{2,1,0:T(8,128)(2,1)S(1)} %all_to_all.15.refs_1_), channel_id=1, source_target_pairs={{0,16},{16,0},{1,17},{17,1},{2,18},{18,2},{3,19},{19,3},{4,20},{20... | collective-permute-start | bytes 3342344 | tf_op jit(solution)/shard_map/ppermute | solution.py:183
  25.1 0.0 copy-done
  25.1 0.0 copy-start.1
  25.1 4.4 %collective-permute-start.1 = (bf16[272,256]{1,0:T(8,128)(2,1)S(1)}, bf16[272,256]{1,0:T(8,128)(2,1)S(1)}, u32[]{:S(2)}, u32[]{:S(2)}) collective-permute-start(bf16[272,256]{1,0:T(8,128)(2,1)S(1)} %copy-done), channel_id=1, source_target_pairs={{0,384},{128,0},{256,128},{384,256},{1,385},{129,1},{257,129},{385... | collective-permute-start | bytes 417800 | tf_op jit(solution)/shard_map/ppermute | solution.py:181
  29.5 1.9 %collective-permute-start.3 = (bf16[272,256]{1,0:T(8,128)(2,1)S(1)}, bf16[272,256]{1,0:T(8,128)(2,1)S(1)}, u32[]{:S(2)}, u32[]{:S(2)}) collective-permute-start(bf16[272,256]{1,0:T(8,128)(2,1)S(1)} %copy-done), channel_id=1, source_target_pairs={{0,128},{128,256},{256,384},{384,0},{1,129},{129,257},{257,385},{3... | collective-permute-start | bytes 417800 | tf_op jit(solution)/shard_map/ppermute | solution.py:181
  31.4 3.6 %collective-permute-start.2 = (bf16[272,256]{1,0:T(8,128)(2,1)S(1)}, bf16[272,256]{1,0:T(8,128)(2,1)S(1)}, u32[]{:S(2)}, u32[]{:S(2)}) collective-permute-start(bf16[272,256]{1,0:T(8,128)(2,1)S(1)} %copy-done), channel_id=1, source_target_pairs={{0,256},{128,384},{256,0},{384,128},{1,257},{129,385},{257,1},{385... | collective-permute-start | bytes 417800 | tf_op jit(solution)/shard_map/ppermute | solution.py:181
  35.1 0.0 collective-permute-done.1.refs_1_
  35.1 1.2 %shard_map.56.refs_3_ = bf16[512,1024]{1,0:T(8,128)(2,1)S(1)} custom-call(bf16[272,256]{1,0:T(8,128)(2,1)S(1)} %copy-done, bf16[272,256]{1,0:T(8,128)(2,1)S(1)} %collective-permute-done.1.refs_1_), custom_call_target="tpu_custom_call" | custom-call | flops 1000000 | bytes 2000000 | tf_op jit(solution)/shard_map/pallas_call | solution.py:167
  36.3 1.3 %collective-permute-done.3.refs_1_ = bf16[272,256]{1,0:T(8,128)(2,1)S(1)} collective-permute-done((bf16[272,256]{1,0:T(8,128)(2,1)S(1)}, bf16[272,256]{1,0:T(8,128)(2,1)S(1)}, u32[]{:S(2)}, u32[]{:S(2)}) %collective-permute-start.3) | collective-permute-done | bytes 139296 | tf_op jit(solution)/shard_map/ppermute | solution.py:181
  37.5 2.3 %collective-permute-done.2.refs_0_ = bf16[272,256]{1,0:T(8,128)(2,1)S(1)} collective-permute-done((bf16[272,256]{1,0:T(8,128)(2,1)S(1)}, bf16[272,256]{1,0:T(8,128)(2,1)S(1)}, u32[]{:S(2)}, u32[]{:S(2)}) %collective-permute-start.2) | collective-permute-done | bytes 139296 | tf_op jit(solution)/shard_map/ppermute | solution.py:181
  39.8 1.1 %shard_map.57.refs_4_ = bf16[512,1024]{1,0:T(8,128)(2,1)S(1)} custom-call(bf16[272,256]{1,0:T(8,128)(2,1)S(1)} %collective-permute-done.2.refs_0_, bf16[272,256]{1,0:T(8,128)(2,1)S(1)} %collective-permute-done.3.refs_1_), custom_call_target="tpu_custom_call" | custom-call | flops 1000000 | bytes 2000000 | tf_op jit(solution)/shard_map/pallas_call | solution.py:167
  41.0 0.0 collective-permute-done.refs_2_
  41.0 0.0 copy-done.1
  41.0 8.4 %shard_map.58 = bf16[4,4,64,512]{3,2,1,0:T(8,128)(2,1)S(1)} custom-call(s32[1,8,16]{2,1,0:T(8,128)S(1)} %bitcast.4, bf16[4,272,512]{2,1,0:T(8,128)(2,1)S(1)} %all_to_all.15.refs_1_, bf16[4,272,512]{2,1,0:T(8,128)(2,1)S(1)} %collective-permute-done.refs_2_, bf16[512,1024]{1,0:T(8,128)(2,1)S(1)} %shard_map.56.refs_3_, bf16[512,1024]{1,0:T(8,128)(2,1)S(1)} %shard_map.57.refs_4_), custom_call_target="tpu_custom_call" | custom-call | flops 2000000000 | bytes 4000000 | tf_op jit(solution)/shard_map/pallas_call | solution.py:185
  49.3 31.5 %all_to_all.16 = bf16[4,4,64,512]{3,2,1,0:T(8,128)(2,1)S(1)} all-to-all(bf16[4,4,64,512]{3,2,1,0:T(8,128)(2,1)S(1)} %shard_map.58), channel_id=1, replica_groups={{0,1,2,3},{4,5,6,7},{8,9,10,11},{12,13,14,15},{20,21,18,19},{24,25,22,2..., dimensions={0} | all-to-all | bytes 2097152 | tf_op jit(solution)/shard_map/all_to_all | solution.py:205
  80.8 0.2 reduce_sum.24
  81.1 27.3 %all_to_all.17 = bf16[4,64,512]{2,1,0:T(8,128)(2,1)S(1)} all-to-all(bf16[4,64,512]{2,1,0:T(8,128)(2,1)S(1)} %reduce_sum.24), channel_id=1, replica_groups={{0,4,8,12},{1,5,9,13},{2,6,10,14},{3,7,11,15},{16,20,24,28},{17,21,25,2..., dimensions={0} | all-to-all | bytes 524288 | tf_op jit(solution)/shard_map/all_to_all | solution.py:207
  108.4 0.7 reduce_sum.25
Async XLA Ops:
  2.1 23.0 %copy-start = (bf16[272,256]{1,0:T(8,128)(2,1)S(1)}, bf16[272,256]{1,0:T(8,128)(2,1)}, u32[]{:S(2)}) copy-start(bf16[272,256]{1,0:T(8,128)(2,1)} %get-tuple-element.8.refs_0_) | copy-start | bytes 417796
  21.1 19.9 %collective-permute-start = (bf16[4,272,512]{2,1,0:T(8,128)(2,1)S(1)}, bf16[4,272,512]{2,1,0:T(8,128)(2,1)S(1)}, u32[]{:S(2)}, u32[]{:S(2)}) collective-permute-start(bf16[4,272,512]{2,1,0:T(8,128)(2,1)S(1)} %all_to_all.15.refs_1_), channel_id=1, source_target_pairs={{0,16},{16,0},{1,17},{17,1},{2,18},{18,2},{3,19},{19,3},{4,20},{20... | collective-permute-start | bytes 3342344 | tf_op jit(solution)/shard_map/ppermute | solution.py:183
  25.1 15.9 %copy-start.1 = (s32[1,16,8]{1,2,0:T(8,128)S(1)}, s32[1,16,8]{1,2,0:T(8,128)}, u32[]{:S(2)}) copy-start(s32[1,16,8]{1,2,0:T(8,128)} %param.9) | copy-start | bytes 1540
  25.1 10.0 %collective-permute-start.1 = (bf16[272,256]{1,0:T(8,128)(2,1)S(1)}, bf16[272,256]{1,0:T(8,128)(2,1)S(1)}, u32[]{:S(2)}, u32[]{:S(2)}) collective-permute-start(bf16[272,256]{1,0:T(8,128)(2,1)S(1)} %copy-done), channel_id=1, source_target_pairs={{0,384},{128,0},{256,128},{384,256},{1,385},{129,1},{257,129},{385... | collective-permute-start | bytes 417800 | tf_op jit(solution)/shard_map/ppermute | solution.py:181
  29.5 8.0 %collective-permute-start.3 = (bf16[272,256]{1,0:T(8,128)(2,1)S(1)}, bf16[272,256]{1,0:T(8,128)(2,1)S(1)}, u32[]{:S(2)}, u32[]{:S(2)}) collective-permute-start(bf16[272,256]{1,0:T(8,128)(2,1)S(1)} %copy-done), channel_id=1, source_target_pairs={{0,128},{128,256},{256,384},{384,0},{1,129},{129,257},{257,385},{3... | collective-permute-start | bytes 417800 | tf_op jit(solution)/shard_map/ppermute | solution.py:181
  31.4 8.4 %collective-permute-start.2 = (bf16[272,256]{1,0:T(8,128)(2,1)S(1)}, bf16[272,256]{1,0:T(8,128)(2,1)S(1)}, u32[]{:S(2)}, u32[]{:S(2)}) collective-permute-start(bf16[272,256]{1,0:T(8,128)(2,1)S(1)} %copy-done), channel_id=1, source_target_pairs={{0,256},{128,384},{256,0},{384,128},{1,257},{129,385},{257,1},{385... | collective-permute-start | bytes 417800 | tf_op jit(solution)/shard_map/ppermute | solution.py:181

commit v4 on v3

--- a/solution.py
+++ b/solution.py
@@ -21,19 +21,11 @@
 SMALL = 8 * 1024 * 1024
 SHIFTS = ((0, 3), (2, 1))
 HALF = 2
+BATCH = 4
 STEP = 16
 VMEM = pl.BlockSpec(memory_space=pltpu.VMEM)
 SMEM = pl.BlockSpec(memory_space=pltpu.SMEM)
 HBM = pl.BlockSpec(memory_space=pltpu.HBM)
-
-
-def repeat(count, unroll, step):
-    def several(t, _):
-        for u in range(unroll):
-            step(t * unroll + u)
-        return 0
-
-    lax.fori_loop(0, count // unroll, several, 0)
 
 
 def head_row(values):
@@ -106,48 +98,46 @@
                     wide[first : first + STEP, pair * PAIR : (pair + 1) * PAIR] = acc.astype(jnp.bfloat16)
 
 
-def product_kernel(near, c_cols, a_own, a_other, wide_first, wide_second, out, rows, full):
+def gather_rows(a_ref, rows):
+    sources = [source_of(shift, "row") for shifts in SHIFTS for shift in shifts]
+    for src in range(a_ref.shape[0]):
+        head = a_ref[src, BODY:, :PAIR].astype(jnp.float32)
+        for j in range(OWN):
+            row = (src * OWN + j) * BLK
+            for s in range(SEC):
+                masks = masks_of(head, (s * OWN + j) * KS, KS, sources)
+                for g in range(BLK // STEP):
+                    first = (s * OWN + j) * BLK + g * STEP
+                    copies = copies_of(a_ref[src, first : first + STEP, :])
+                    for pair in range(IBS // OWN):
+                        acc = jnp.where(masks[pair][0], copies[0], 0.0)
+                        for k in range(1, KS):
+                            acc = acc + jnp.where(masks[pair][k], copies[k], 0.0)
+                        lane = ((pair // HALF * SEC + s) * HALF + pair % HALF) * PAIR
+                        rows[row + g * STEP : row + (g + 1) * STEP, lane : lane + PAIR] = acc.astype(jnp.bfloat16)
+
+
+def product_kernel(near, c_cols, rows_own, a_other, wide_first, wide_second, out, rows_other, *fulls):
     core = lax.axis_index("core")
-    parts = a_own.shape[0]
-    sources = [[source_of(shift, "row") for shift in shifts] for shifts in SHIFTS]
-    for side, a_ref in enumerate((a_own, a_other)):
-
-        def gather(src, side=side, a_ref=a_ref):
-            head = a_ref[src, BODY:, :PAIR].astype(jnp.float32)
-            for j in range(OWN):
-                row = pl.multiple_of(((side * parts + src) * OWN + j) * BLK, BLK)
-                for s in range(SEC):
-                    masks = masks_of(head, (s * OWN + j) * KS, KS, sources[0] + sources[1])
-                    for g in range(BLK // STEP):
-                        first = (s * OWN + j) * BLK + g * STEP
-                        copies = copies_of(a_ref[src, first : first + STEP, :])
-                        for pair in range(IBS // OWN):
-                            acc = jnp.where(masks[pair][0], copies[0], 0.0)
-                            for k in range(1, KS):
-                                acc = acc + jnp.where(masks[pair][k], copies[k], 0.0)
-                            lane = ((pair // HALF * SEC + s) * HALF + pair % HALF) * PAIR
-                            rows[pl.ds(row + g * STEP, STEP), lane : lane + PAIR] = acc.astype(jnp.bfloat16)
-
-        repeat(parts, 2, gather)
-
-    wide = jnp.concatenate([wide_first[...], wide_second[...]], axis=0)
-    full[...] = jnp.dot(rows[...], wide, preferred_element_type=jnp.float32).astype(jnp.bfloat16)
+    block_rows = rows_own.shape[0] // BLK
     low = lax.broadcasted_iota(jnp.int32, (BLK, PAIR), 1).astype(jnp.int16) < jnp.int16(BLK)
-    for side in range(CORES):
+    for side, (rows, full) in enumerate(zip((rows_own, rows_other), fulls)):
         owner = core if side == 0 else 1 - core
-
-        def pick(n, side=side, owner=owner):
-            i = (n // OWN * CORES + owner) * OWN + lax.rem(n, OWN)
-            row = pl.multiple_of((side * parts * OWN + n) * BLK, BLK)
+        if side == 1:
+            gather_rows(a_other, rows_other)
+        for n in range(block_rows):
+            if n % BATCH == 0:
+                part = slice(n * BLK, (n + BATCH) * BLK)
+                wide = jnp.concatenate([wide_first[...], wide_second[...]], axis=0)
+                full[part] = jnp.dot(rows[part], wide, preferred_element_type=jnp.float32).astype(jnp.bfloat16)
+            i = (n // OWN * CORES + owner) * OWN + n % OWN
             for pair in range(KC // 2):
                 picked = []
                 for m in range(2):
                     c = c_cols[0, pair * 2 + m, i]
-                    two = full[pl.ds(row, BLK), pl.ds(pl.multiple_of(c // 2 * PAIR, PAIR), PAIR)]
+                    two = full[n * BLK : (n + 1) * BLK, pl.ds(pl.multiple_of(c // 2 * PAIR, PAIR), PAIR)]
                     picked.append(jnp.where(lax.rem(c, 2) == m, two, swap(two)))
                 out[lax.rem(i, near), i // near, :, pair * PAIR : (pair + 1) * PAIR] = jnp.where(low, *picked)
-
-        repeat(parts * OWN, 8, pick)
 
 
 def local(a_blocks, a_cols, p_blocks, p_cols, c_cols):
@@ -181,6 +171,14 @@
     p_parts = [p_out] + [lax.ppermute(p_out, "row", [(i, (i + d) % rows) for i in range(rows)]) for d in range(1, rows)]
     first = expand(*[p_parts[d] for d in SHIFTS[0]])
     a_other = lax.ppermute(a_own, "core", [(0, 1), (1, 0)])
+    rows_own = pl.pallas_call(
+        gather_rows,
+        out_shape=jax.ShapeDtypeStruct((chips * OWN * BLK, SEC * IBS * BLK), jnp.bfloat16),
+        in_specs=[VMEM],
+        out_specs=VMEM,
+        cost_estimate=pl.CostEstimate(flops=10**6, bytes_accessed=2 * 10**6, transcendentals=0),
+        compiler_params=pltpu.CompilerParams(vmem_limit_bytes=SMALL),
+    )(a_own)
     second = expand(*[p_parts[d] for d in SHIFTS[1]])
     partial = pl.pallas_call(
         lambda *refs: product_kernel(near, *refs),
@@ -188,12 +186,13 @@
         in_specs=[SMEM] + [VMEM] * 4,
         out_specs=VMEM,
         scratch_shapes=[
-            pltpu.VMEM((chips * CORES * OWN * BLK, SEC * IBS * BLK), jnp.bfloat16),
-            pltpu.VMEM((chips * CORES * OWN * BLK, NCC * BLK), jnp.bfloat16),
+            pltpu.VMEM((chips * OWN * BLK, SEC * IBS * BLK), jnp.bfloat16),
+            pltpu.VMEM((chips * OWN * BLK, NCC * BLK), jnp.bfloat16),
+            pltpu.VMEM((chips * OWN * BLK, NCC * BLK), jnp.bfloat16),
         ],
         cost_estimate=pl.CostEstimate(flops=2 * 10**9, bytes_accessed=4 * 10**6, transcendentals=0),
         compiler_params=pltpu.CompilerParams(vmem_limit_bytes=3 * SMALL),
-    )(c_cols.transpose(0, 2, 1), a_own, a_other, first, second)
+    )(c_cols.transpose(0, 2, 1), rows_own, a_other, first, second)
 
     def group(core, g):
         first = near * g + (near // 2) * core

time: 109 us -> 110 us (level)
  waiting for transfers between devices: 3.56 us -> 5.46 us
    pallas_call x1, Pallas kernels: 8.35 us -> 5.38 us  [local(): pl.pallas_call(lambda *refs: product_kernel(near, *refs), out_shape=jax.S...]
    pallas_call x0 -> x1, Pallas kernels: none -> 2.07 us  [local(): pl.pallas_call(gather_rows, out_shape=jax.ShapeDtypeStruct((chips * OWN *...]
    ppermute x3, waiting for transfers between devices: 3.56 us -> 5.46 us  [local(): lax.ppermute(p_out, 'row', [(i, (i + d) % rows) for i in range(rows)])]
  transfers between devices with their start and end apart: 4 -> 4, of which waited for: 2 -> 2; matrix products, arithmetic and copies ran while one was open for 0% -> 0% of each run, Pallas kernels for 2% -> 4%
where the time goes in v4:
time: 110 us; the launch traced here: 109 us
  blocking collectives  77.8 us (71%)
  starting transfers between devices  13.3 us (12%)
  Pallas kernels  11.9 us (11%)
  waiting for transfers between devices  5.46 us (5%)
    all_to_all x1, blocking collectives, local(): lax.all_to_all(partial, ('core', 'layer'), 0, 0, axis_index_groups=close,...  31.5 us
    all_to_all x1, blocking collectives, local(): got = lax.all_to_all(part, 'layer', 0, 0, axis_index_groups=far, tiled=True)  27.3 us
    all_to_all x1, blocking collectives, local(): a_own = lax.all_to_all(a_out, 'chip', 0, 0, tiled=True)  19 us
    ppermute x3, starting transfers between devices, local(): lax.ppermute(p_out, 'row', [(i, (i + d) % rows) for i in range(rows)])  9.33 us
    ppermute x3, waiting for transfers between devices, local(): lax.ppermute(p_out, 'row', [(i, (i + d) % rows) for i in range(rows)])  5.46 us
    pallas_call x1, Pallas kernels, local(): pl.pallas_call(lambda *refs: product_kernel(near, *refs), out_shape=jax.S...  5.38 us
    ppermute x1, starting transfers between devices, local(): a_other = lax.ppermute(a_own, 'core', [(0, 1), (1, 0)])  4 us
    pallas_call x2, Pallas kernels, expand(): pl.pallas_call(expand_kernel, out_shape=jax.ShapeDtypeStruct((HALF * SEC...  2.32 us
  transfers between devices with their start and end apart: 4, of which 2 were waited for; matrix products, arithmetic and copies ran while one was open for 0% of the time, Pallas kernels for 4%

profile of v4, /device:TPU:33, one launch (start us, length us, event | category | flops | bytes accessed | tf_op | source)
XLA Modules:
  0.0 109.4 jit_solution(13628360609907116029)
XLA Ops:
  0.0 2.1 %shard_map.55 = (bf16[4,272,512]{2,1,0:T(8,128)(2,1)}, bf16[272,256]{1,0:T(8,128)(2,1)}) custom-call(s32[1,2,2,8]{3,2,1,0:T(2,128)} %a_cols.1, s32[1,2,1,2,4]{4,3,2,1,0:T(2,128)} %p_cols.1, bf16[256,512]{1,0:T(8,128)(2,1)} %bitcast.5, bf16[256,256]{1,0:T(8,128)(2,1)} %bitcast.6), custom_call_target="tpu_custom_call" | custom-call | tf_op jit(solution)/shard_map/pallas_call | solution.py:146
  2.1 0.0 copy-start
  2.1 19.0 %all_to_all.15.a_ref = bf16[4,272,512]{2,1,0:T(8,128)(2,1)S(1)} all-to-all(bf16[4,272,512]{2,1,0:T(8,128)(2,1)} %get-tuple-element.7), channel_id=1, replica_groups=mesh['row'=4,'chip'=4,'core'=2,'layer'=16] {'chip'}, dimensions={0} | all-to-all | bytes 2228224 | tf_op jit(solution)/shard_map/all_to_all | solution.py:170
  21.1 4.0 %collective-permute-start = (bf16[4,272,512]{2,1,0:T(8,128)(2,1)S(1)}, bf16[4,272,512]{2,1,0:T(8,128)(2,1)S(1)}, u32[]{:S(2)}, u32[]{:S(2)}) collective-permute-start(bf16[4,272,512]{2,1,0:T(8,128)(2,1)S(1)} %all_to_all.15.a_ref), channel_id=1, source_target_pairs={{0,16},{16,0},{1,17},{17,1},{2,18},{18,2},{3,19},{19,3},{4,20},{20... | collective-permute-start | bytes 3342344 | tf_op jit(solution)/shard_map/ppermute | solution.py:173
  25.1 0.0 copy-done
  25.1 4.4 %collective-permute-start.1 = (bf16[272,256]{1,0:T(8,128)(2,1)S(1)}, bf16[272,256]{1,0:T(8,128)(2,1)S(1)}, u32[]{:S(2)}, u32[]{:S(2)}) collective-permute-start(bf16[272,256]{1,0:T(8,128)(2,1)S(1)} %copy-done), channel_id=1, source_target_pairs={{0,384},{128,0},{256,128},{384,256},{1,385},{129,1},{257,129},{385... | collective-permute-start | bytes 417800 | tf_op jit(solution)/shard_map/ppermute | solution.py:171
  29.5 2.4 %collective-permute-start.2 = (bf16[272,256]{1,0:T(8,128)(2,1)S(1)}, bf16[272,256]{1,0:T(8,128)(2,1)S(1)}, u32[]{:S(2)}, u32[]{:S(2)}) collective-permute-start(bf16[272,256]{1,0:T(8,128)(2,1)S(1)} %copy-done), channel_id=1, source_target_pairs={{0,256},{128,384},{256,0},{384,128},{1,257},{129,385},{257,1},{385... | collective-permute-start | bytes 417800 | tf_op jit(solution)/shard_map/ppermute | solution.py:171
  31.9 2.5 %collective-permute-start.3 = (bf16[272,256]{1,0:T(8,128)(2,1)S(1)}, bf16[272,256]{1,0:T(8,128)(2,1)S(1)}, u32[]{:S(2)}, u32[]{:S(2)}) collective-permute-start(bf16[272,256]{1,0:T(8,128)(2,1)S(1)} %copy-done), channel_id=1, source_target_pairs={{0,128},{128,256},{256,384},{384,0},{1,129},{129,257},{257,385},{3... | collective-permute-start | bytes 417800 | tf_op jit(solution)/shard_map/ppermute | solution.py:171
  34.5 0.0 collective-permute-done.1.refs_1_
  34.5 1.2 %shard_map.57.refs_3_ = bf16[512,1024]{1,0:T(8,128)(2,1)S(1)} custom-call(bf16[272,256]{1,0:T(8,128)(2,1)S(1)} %copy-done, bf16[272,256]{1,0:T(8,128)(2,1)S(1)} %collective-permute-done.1.refs_1_), custom_call_target="tpu_custom_call" | custom-call | flops 1000000 | bytes 2000000 | tf_op jit(solution)/shard_map/pallas_call | solution.py:157
  35.6 2.2 %collective-permute-done.2.refs_0_ = bf16[272,256]{1,0:T(8,128)(2,1)S(1)} collective-permute-done((bf16[272,256]{1,0:T(8,128)(2,1)S(1)}, bf16[272,256]{1,0:T(8,128)(2,1)S(1)}, u32[]{:S(2)}, u32[]{:S(2)}) %collective-permute-start.2) | collective-permute-done | bytes 139296 | tf_op jit(solution)/shard_map/ppermute | solution.py:171
  37.8 3.3 %collective-permute-done.3.refs_1_ = bf16[272,256]{1,0:T(8,128)(2,1)S(1)} collective-permute-done((bf16[272,256]{1,0:T(8,128)(2,1)S(1)}, bf16[272,256]{1,0:T(8,128)(2,1)S(1)}, u32[]{:S(2)}, u32[]{:S(2)}) %collective-permute-start.3) | collective-permute-done | bytes 139296 | tf_op jit(solution)/shard_map/ppermute | solution.py:171
  41.1 1.1 %shard_map.58.refs_4_ = bf16[512,1024]{1,0:T(8,128)(2,1)S(1)} custom-call(bf16[272,256]{1,0:T(8,128)(2,1)S(1)} %collective-permute-done.2.refs_0_, bf16[272,256]{1,0:T(8,128)(2,1)S(1)} %collective-permute-done.3.refs_1_), custom_call_target="tpu_custom_call" | custom-call | flops 1000000 | bytes 2000000 | tf_op jit(solution)/shard_map/pallas_call | solution.py:157
  42.2 0.0 copy-start.1
  42.3 2.1 %shard_map.56.refs_1_ = bf16[512,1024]{1,0:T(8,128)(2,1)S(1)} custom-call(bf16[4,272,512]{2,1,0:T(8,128)(2,1)S(1)} %all_to_all.15.a_ref), custom_call_target="tpu_custom_call" | custom-call | flops 1000000 | bytes 2000000 | tf_op jit(solution)/shard_map/pallas_call | solution.py:174
  44.3 0.0 collective-permute-done.refs_2_
  44.3 0.0 copy-done.1
  44.4 5.4 %shard_map.59 = bf16[4,4,64,512]{3,2,1,0:T(8,128)(2,1)S(1)} custom-call(s32[1,8,16]{2,1,0:T(8,128)S(1)} %bitcast.4, bf16[512,1024]{1,0:T(8,128)(2,1)S(1)} %shard_map.56.refs_1_, bf16[4,272,512]{2,1,0:T(8,128)(2,1)S(1)} %collective-permute-done.refs_2_, bf16[512,1024]{1,0:T(8,128)(2,1)S(1)} %shard_map.57.refs_3_, bf16[512,1024]{1,0:T(8,128)(2,1)S(1)} %shard_map.58.refs_4_), custom_call_target="tpu_custom_call" | custom-call | flops 2000000000 | bytes 4000000 | tf_op jit(solution)/shard_map/pallas_call | solution.py:183
  49.7 31.5 %all_to_all.16 = bf16[4,4,64,512]{3,2,1,0:T(8,128)(2,1)S(1)} all-to-all(bf16[4,4,64,512]{3,2,1,0:T(8,128)(2,1)S(1)} %shard_map.59), channel_id=1, replica_groups={{0,1,2,3},{4,5,6,7},{8,9,10,11},{12,13,14,15},{20,21,18,19},{24,25,22,2..., dimensions={0} | all-to-all | bytes 2097152 | tf_op jit(solution)/shard_map/all_to_all | solution.py:204
  81.3 0.2 reduce_sum.24
  81.5 27.3 %all_to_all.17 = bf16[4,64,512]{2,1,0:T(8,128)(2,1)S(1)} all-to-all(bf16[4,64,512]{2,1,0:T(8,128)(2,1)S(1)} %reduce_sum.24), channel_id=1, replica_groups={{0,4,8,12},{1,5,9,13},{2,6,10,14},{3,7,11,15},{16,20,24,28},{17,21,25,2..., dimensions={0} | all-to-all | bytes 524288 | tf_op jit(solution)/shard_map/all_to_all | solution.py:206
  108.8 0.7 reduce_sum.25
Async XLA Ops:
  2.1 23.0 %copy-start = (bf16[272,256]{1,0:T(8,128)(2,1)S(1)}, bf16[272,256]{1,0:T(8,128)(2,1)}, u32[]{:S(2)}) copy-start(bf16[272,256]{1,0:T(8,128)(2,1)} %get-tuple-element.8.refs_0_) | copy-start | bytes 417796
  21.1 23.3 %collective-permute-start = (bf16[4,272,512]{2,1,0:T(8,128)(2,1)S(1)}, bf16[4,272,512]{2,1,0:T(8,128)(2,1)S(1)}, u32[]{:S(2)}, u32[]{:S(2)}) collective-permute-start(bf16[4,272,512]{2,1,0:T(8,128)(2,1)S(1)} %all_to_all.15.a_ref), channel_id=1, source_target_pairs={{0,16},{16,0},{1,17},{17,1},{2,18},{18,2},{3,19},{19,3},{4,20},{20... | collective-permute-start | bytes 3342344 | tf_op jit(solution)/shard_map/ppermute | solution.py:173
  25.1 9.4 %collective-permute-start.1 = (bf16[272,256]{1,0:T(8,128)(2,1)S(1)}, bf16[272,256]{1,0:T(8,128)(2,1)S(1)}, u32[]{:S(2)}, u32[]{:S(2)}) collective-permute-start(bf16[272,256]{1,0:T(8,128)(2,1)S(1)} %copy-done), channel_id=1, source_target_pairs={{0,384},{128,0},{256,128},{384,256},{1,385},{129,1},{257,129},{385... | collective-permute-start | bytes 417800 | tf_op jit(solution)/shard_map/ppermute | solution.py:171
  29.5 8.3 %collective-permute-start.2 = (bf16[272,256]{1,0:T(8,128)(2,1)S(1)}, bf16[272,256]{1,0:T(8,128)(2,1)S(1)}, u32[]{:S(2)}, u32[]{:S(2)}) collective-permute-start(bf16[272,256]{1,0:T(8,128)(2,1)S(1)} %copy-done), channel_id=1, source_target_pairs={{0,256},{128,384},{256,0},{384,128},{1,257},{129,385},{257,1},{385... | collective-permute-start | bytes 417800 | tf_op jit(solution)/shard_map/ppermute | solution.py:171
  31.9 9.2 %collective-permute-start.3 = (bf16[272,256]{1,0:T(8,128)(2,1)S(1)}, bf16[272,256]{1,0:T(8,128)(2,1)S(1)}, u32[]{:S(2)}, u32[]{:S(2)}) collective-permute-start(bf16[272,256]{1,0:T(8,128)(2,1)S(1)} %copy-done), channel_id=1, source_target_pairs={{0,128},{128,256},{256,384},{384,0},{1,129},{129,257},{257,385},{3... | collective-permute-start | bytes 417800 | tf_op jit(solution)/shard_map/ppermute | solution.py:171
  42.2 2.1 %copy-start.1 = (s32[1,16,8]{1,2,0:T(8,128)S(1)}, s32[1,16,8]{1,2,0:T(8,128)}, u32[]{:S(2)}) copy-start(s32[1,16,8]{1,2,0:T(8,128)} %param.9) | copy-start | bytes 1540
